TPU v7x, 32 devices: a whole 2x2x4 slice. The times are simulated.
32 devices in a mesh: seq: 16 (over z, y, core), head: 2 (over x).
Axes of the slice: x: 2, y: 2, z: 4, core: 2. Of those that a mesh axis runs over, the one named last changes fastest.
Arguments:
- queries: bfloat16 [4096, 768], P('seq', 'head'), may hold values from -37 to 37
- key_rows: bfloat16 [4096, 768], P('seq', 'head'), may hold values from -4 to 4
- value_rows: bfloat16 [4096, 768], P('seq', 'head'), may hold values from -5 to 5
- out_grad: bfloat16 [4096, 768], P('seq', 'head'), may hold values from -80 to 80
- query_weight: bfloat16 [5120, 768], P('seq', 'head'), may hold values from -0.078125 to 0.078125
- neighbour_tiles: int32 [32, 12], replicated, may hold values from 0 to 31, as said below
- neighbour_count: int32 [32], replicated, may hold values from 1 to 12, as said below
Outputs:
- input_grad: bfloat16 [4096, 5120], P('seq', 'head')
- key_grad: bfloat16 [4096, 768], P('seq', 'head')
- value_grad: bfloat16 [4096, 768], P('seq', 'head')
Inputs may be any that keep to these rules, and one draw needn't show every extreme that they name: `neighbour_tiles`: the first neighbour_count[g] entries of row g are distinct tiles of frames t - 1, t and t + 1, where t is tile g's frame, at most one row and one column away from g, and include g itself; the remaining entries repeat g. `neighbour_count`: some tile has 12 live entries.
All inputs are finite; a program needn't handle non-finite values.
Results may differ from a plain program's by a relative error of at most 0.012.
Values may be sent and summed in bfloat16 or wider, within the bound.
No kernel may reach another device: no remote copies, remote signals or barrier semaphores. Data moves between devices by JAX's collectives and lax.ppermute only.
A program may use at most 64 MiB of HBM per device.

v0:
```python
import jax
import jax.numpy as jnp
from jax import lax
from jax.experimental import pallas as pl
from jax.experimental.pallas import tpu as pltpu
from jax.sharding import PartitionSpec as P

HEAD_DIM = 128
HEADS_DEV = 3
TILE = 128
TILES_DEV = 2
SCALE = HEAD_DIM ** (-0.5)
LOG2_E = 1.4426950408889634
SCALE_2 = SCALE * LOG2_E
BLOCKS = 6
DEAD = -64


def move(block, route):
    size = lax.axis_size("seq")
    pairs = [(i, route(i)) for i in range(size)]
    return lax.ppermute(block, "seq", [(i, j) for i, j in pairs if 0 <= j < size])


def swap_groups(block):
    return lax.ppermute(block, "head", [(0, 1), (1, 0)])


def to_core(i):
    return i ^ 1


def to_frame_pair(i):
    return i ^ 2


def to_next_pair(i):
    return i + 4 if i % 4 < 2 else i - 4


def owners(position):
    far = jnp.where(position % 4 < 2, position - 2, position + 2)
    return [position, position ^ 1, position ^ 2, position ^ 3, far, far ^ 1]


def nt(left, right):
    return lax.dot_general(
        left, right, (((1,), (1,)), ((), ())), preferred_element_type=jnp.float32
    )


def tn(left, right):
    return lax.dot_general(
        left, right, (((0,), (0,)), ((), ())), preferred_element_type=jnp.float32
    )


def any_lane(hits):
    best = jnp.max(jnp.where(hits, 1.0, 0.0), axis=1, keepdims=True)
    return jnp.where(best > 0.0, 0.0, -jnp.inf)


def own_query_masks(position, lists_ref, mask_ref):
    row = lax.broadcasted_iota(jnp.int32, (16, lists_ref.shape[1]), 0)
    tile = jnp.full(row.shape, 2 * DEAD, jnp.int32)
    for b, owner in enumerate(owners(position)):
        tile = jnp.where(row // TILES_DEV == b, owner * TILES_DEV + row % TILES_DEV, tile)
    for c in range(TILES_DEV):
        own = lists_ref[pl.ds(position * TILES_DEV + c, 1)]
        mask_ref[c] = jnp.broadcast_to(any_lane(own == tile), mask_ref.shape[1:])


def own_key_masks(position, lists_ref, mask_ref):
    for a in range(TILES_DEV):
        hits = lists_ref[...] == position * TILES_DEV + a
        mask_ref[a] = jnp.broadcast_to(any_lane(hits), mask_ref.shape[1:])


def query_kernel(
    at_ref, lists_ref, q_ref, g_ref, k_ref, v_ref, b1, b2, b3, b4, b5,
    dq_ref, stat_ref, s_ref, d_ref, mask_ref,
):
    own_query_masks(at_ref[0], lists_ref, mask_ref)
    stat_ref[...] = jnp.zeros_like(stat_ref)
    half = q_ref.shape[0] // TILES_DEV
    pairs = [b1, b2, b3, b4, b5]
    tiles = [(b, a) for b in range(BLOCKS) for a in range(TILES_DEV)]

    def mask(b, a):
        at = TILES_DEV * b + a
        return jnp.concatenate([mask_ref[0, at : at + 1], mask_ref[1, at : at + 1]], axis=1)

    for head in range(HEADS_DEV):
        cols = slice(head * HEAD_DIM, (head + 1) * HEAD_DIM)
        query = q_ref[:, cols]
        grad = g_ref[:, cols]

        def key(b):
            return k_ref[:, cols] if b == 0 else pairs[b - 1][0, :, cols]

        def value(b):
            return v_ref[:, cols] if b == 0 else pairs[b - 1][1, :, cols]

        top = None
        for b in range(BLOCKS):
            scores = nt(key(b), query)
            s_ref[b] = scores
            d_ref[b] = nt(value(b), grad)
            for a in range(TILES_DEV):
                peak = jnp.max(scores[a * half : (a + 1) * half], axis=0, keepdims=True)
                peak = peak * SCALE_2 + mask(b, a)
                top = peak if top is None else jnp.maximum(top, peak)
        total = jnp.zeros_like(top)
        delta = jnp.zeros_like(top)
        for b, a in tiles:
            part = slice(a * half, (a + 1) * half)
            weight = jnp.exp2(s_ref[b, part] * SCALE_2 - (top - mask(b, a)))
            s_ref[b, part] = weight
            total = total + jnp.sum(weight, axis=0, keepdims=True)
            delta = delta + jnp.sum(weight * d_ref[b, part], axis=0, keepdims=True)
        inverse = 1.0 / total
        delta = delta * inverse
        acc = jnp.zeros((HEAD_DIM, query.shape[0]), jnp.float32)
        for b in range(BLOCKS):
            dscores = (s_ref[b] * (d_ref[b] - delta)).astype(jnp.bfloat16)
            acc = acc + tn(key(b), dscores)
        dq_ref[:, cols] = (acc * (inverse * SCALE)).T.astype(jnp.bfloat16)
        stat_ref[head : head + 1] = top + jnp.log(total) * LOG2_E
        stat_ref[head + HEADS_DEV : head + HEADS_DEV + 1] = delta


def key_kernel(
    at_ref, lists_ref, k_ref, v_ref, q_ref, g_ref, b1, b2, b3, b4, b5,
    t0, t1, t2, t4, dk_ref, dv_ref, mask_ref,
):
    tiles = lists_ref.shape[0]
    own_key_masks(at_ref[0], lists_ref, mask_ref)
    half = k_ref.shape[0] // TILES_DEV
    pairs = [b1, b2, b3, b4, b5]
    stats = [(t0, 0), (t1, 0), (t2, 0), (t2, 8), (t4, 0), (t4, 8)]
    masks = []
    for owner in owners(at_ref[0]):
        first = owner * TILES_DEV
        inside = (first >= 0) & (first < tiles)
        there = jnp.where(inside, 0.0, -jnp.inf)
        row = jnp.where(inside, first, 0)
        masks.append([
            jnp.concatenate([mask_ref[a, pl.ds(row + c, 1)] for c in range(TILES_DEV)], axis=1)
            + there
            for a in range(TILES_DEV)
        ])
    for head in range(HEADS_DEV):
        cols = slice(head * HEAD_DIM, (head + 1) * HEAD_DIM)
        key = k_ref[:, cols]
        value = v_ref[:, cols]
        key_acc = jnp.zeros(key.shape, jnp.float32)
        value_acc = jnp.zeros(key.shape, jnp.float32)
        for b in range(BLOCKS):
            query = q_ref[:, cols] if b == 0 else pairs[b - 1][0, :, cols]
            grad = g_ref[:, cols] if b == 0 else pairs[b - 1][1, :, cols]
            stat, at = stats[b]
            log_norm = stat[at + head : at + head + 1]
            at += HEADS_DEV
            delta = stat[at + head : at + head + 1]
            scores = nt(key, query)
            dprobs = nt(value, grad)
            low, dscores = [], []
            for a in range(TILES_DEV):
                part = slice(a * half, (a + 1) * half)
                probs = jnp.exp2(scores[part] * SCALE_2 - (log_norm - masks[b][a]))
                low.append(probs.astype(jnp.bfloat16))
                dscores.append((probs * (dprobs[part] - delta)).astype(jnp.bfloat16))
            low = jnp.concatenate(low, axis=0)
            dscores = jnp.concatenate(dscores, axis=0)
            value_acc = value_acc + jnp.dot(low, grad, preferred_element_type=jnp.float32)
            key_acc = key_acc + jnp.dot(dscores, query, preferred_element_type=jnp.float32)
        dk_ref[:, cols] = (key_acc * SCALE).astype(jnp.bfloat16)
        dv_ref[:, cols] = value_acc.astype(jnp.bfloat16)


SMEM = pl.BlockSpec(memory_space=pltpu.SMEM)
VMEM = pl.BlockSpec(memory_space=pltpu.VMEM)
ANYWHERE = pl.BlockSpec(memory_space=pl.ANY)


def query_pass(at, lists, queries, out_grad, keys, values, pairs):
    rows, width = queries.shape
    return pl.pallas_call(
        query_kernel,
        in_specs=[SMEM] + [VMEM] * 10,
        out_specs=[VMEM] * 2,
        out_shape=[
            jax.ShapeDtypeStruct((rows, width), jnp.bfloat16),
            jax.ShapeDtypeStruct((8, rows), jnp.float32),
        ],
        scratch_shapes=[pltpu.VMEM((BLOCKS, rows, rows), jnp.float32)] * 2
        + [pltpu.VMEM((TILES_DEV, 16, TILE), jnp.float32)],
        name="query_pass",
    )(at, lists, queries, out_grad, keys, values, *pairs)


def key_pass(at, lists, keys, values, queries, out_grad, pairs, stats):
    rows, width = queries.shape
    return pl.pallas_call(
        key_kernel,
        in_specs=[SMEM] + [VMEM] * 14,
        out_specs=[VMEM] * 2,
        out_shape=[jax.ShapeDtypeStruct((rows, width), jnp.bfloat16)] * 2,
        scratch_shapes=[pltpu.VMEM((TILES_DEV, lists.shape[0], TILE), jnp.float32)],
        name="key_pass",
    )(at, lists, keys, values, queries, out_grad, *pairs, *stats)


def pack_kernel(slots_ref, counts_ref, k_ref, v_ref, q_ref, g_ref, kv_ref, qg_ref, lists_ref):
    kv_ref[0] = k_ref[...]
    kv_ref[1] = v_ref[...]
    qg_ref[0] = q_ref[...]
    qg_ref[1] = g_ref[...]
    slots, tiles = slots_ref.shape
    side = 128
    for first in range(0, tiles, side):
        width = min(side, tiles - first)
        block = slots_ref[:, first : first + width]
        used = lax.broadcasted_iota(jnp.int32, block.shape, 0) < counts_ref[:, first : first + width]
        block = jnp.where(used, block, DEAD)
        block = jnp.concatenate([block, jnp.full((16 - slots, width), DEAD, jnp.int32)], axis=0)
        if width < side:
            block = jnp.concatenate([block, jnp.full((16, side - width), DEAD, jnp.int32)], axis=1)
        block = jnp.concatenate([block, jnp.full((side - 16, side), DEAD, jnp.int32)], axis=0)
        lists_ref[first : first + width] = block.T[:width]


def pack(slots, counts, keys, values, queries, out_grad):
    pair = jax.ShapeDtypeStruct((2,) + keys.shape, keys.dtype)
    return pl.pallas_call(
        pack_kernel,
        in_specs=[VMEM] * 6,
        out_specs=[VMEM] * 3,
        out_shape=[pair, pair, jax.ShapeDtypeStruct((slots.shape[1], 128), jnp.int32)],
        name="pack",
    )(slots, counts, keys, values, queries, out_grad)


def start_input(at_ref, pieces, w_ref, sems):
    rows = pieces[0].shape[1]
    copies = []
    for j in range(2):
        for i, piece in enumerate(pieces):
            place = (at_ref[0] % 4) ^ (i % 4)
            copy = pltpu.make_async_copy(
                piece.at[j],
                w_ref.at[j, i // 4, pl.ds(pl.multiple_of(place * rows, 64), rows)],
                sems.at[8 * j + i],
            )
            copy.start()
            copies.append(copy)
    return copies


def finish_input(at_ref, q_ref, x_ref, copies, w_ref, o_ref, out_ref, sems):
    span = w_ref.shape[2]
    own = q_ref[...]
    other = x_ref[...]
    outs = []
    for j in range(2):
        for copy in copies[8 * j : 8 * j + 8]:
            copy.wait()
        part = nt(own, w_ref[j, 0]) + nt(other, w_ref[j, 1])
        o_ref[j] = part.astype(o_ref.dtype)
        first = pl.multiple_of((at_ref[0] % 8 // 4 ^ j) * span, span)
        copy = pltpu.make_async_copy(o_ref.at[j], out_ref.at[:, pl.ds(first, span)], sems.at[j])
        copy.start()
        outs.append(copy)
    for copy in outs:
        copy.wait()


def input_kernel(at_ref, own_ref, other_ref, *refs):
    pieces = refs[:8]
    out_ref, w_ref, o_ref, sems, out_sems = refs[8:]
    copies = start_input(at_ref, pieces, w_ref, sems)
    finish_input(at_ref, own_ref, other_ref, copies, w_ref, o_ref, out_ref, out_sems)


def input_pass(at, own, other, pieces):
    rows, width = own.shape
    span = pieces[0].shape[1] * 4
    return pl.pallas_call(
        input_kernel,
        in_specs=[SMEM, VMEM, VMEM] + [ANYWHERE] * 8,
        out_specs=ANYWHERE,
        out_shape=jax.ShapeDtypeStruct((rows, 2 * span), jnp.bfloat16),
        scratch_shapes=[
            pltpu.VMEM((2, 2, span, width), jnp.bfloat16),
            pltpu.VMEM((2, rows, span), jnp.bfloat16),
            pltpu.SemaphoreType.DMA((16,)),
            pltpu.SemaphoreType.DMA((2,)),
        ],
        name="input_pass",
    )(at, own, other, *pieces)


def spread_weight(weight, position, group):
    by_one = move(weight, lambda i: i ^ 4)
    by_two = move(weight, lambda i: i ^ 8)
    middle = move(weight, lambda i: i ^ 12 if 4 <= i < 12 else -1)
    outer = move(by_two, lambda i: i ^ 4 if 4 <= i < 12 else -1)
    by_three = jnp.where((position >= 4) & (position < 12), middle, outer)
    near = jnp.stack([weight, by_one])
    away = jnp.stack([by_two, by_three])
    same = position // 8 == group
    kept = jnp.where(same, near, away)
    sent = jnp.where(same, away, near)
    swapped = swap_groups(sent)
    pieces = []
    for held in (kept, swapped):
        paired = move(held, to_frame_pair)
        core = move(held, to_core)
        pieces += [held, core, paired, move(paired, to_core)]
    return pieces


def input_by_gather(query_grad, weight):
    size, groups = lax.axis_size("seq"), lax.axis_size("head")
    part = size // groups
    route = []
    for p in range(size):
        for c in range(groups):
            high, low = divmod(p, part)
            route.append((p * groups + c, (c * part + low) * groups + high))
    regrouped = lax.ppermute(weight, ("seq", "head"), route)
    gathered = lax.all_gather(regrouped, "seq", axis=0, tiled=True)
    gathered = gathered.reshape(groups, -1, weight.shape[1])
    rows = lax.all_gather(query_grad, "head")
    total = jnp.einsum("grk,gck->rc", rows, gathered, preferred_element_type=jnp.float32)
    return total.astype(jnp.bfloat16)


def gradients(
    queries, key_rows, value_rows, out_grad, query_weight, neighbour_tiles, neighbour_count
):
    position = lax.axis_index("seq")
    direct = lax.axis_size("seq") == 16 and lax.axis_size("head") == 2
    kv_pair, qg_pair, lists = pack(
        neighbour_tiles.T, neighbour_count[None], key_rows, value_rows, queries, out_grad
    )
    if direct:
        pieces = spread_weight(query_weight, position, lax.axis_index("head"))
    at = jnp.full((1,), position, jnp.int32)

    def window(pair):
        near = move(pair, to_frame_pair)
        far = move(near, to_next_pair)
        core = move(pair, to_core)
        near_core = move(near, to_core)
        return [core, near, near_core, far, move(far, to_core)]

    kv_pairs = window(kv_pair)
    qg_pairs = window(qg_pair)
    query_grad, own = query_pass(
        at, lists, queries, out_grad, key_rows, value_rows, kv_pairs
    )
    core = move(own, to_core)
    near = move(jnp.concatenate([own, core]), to_frame_pair)
    stats = [own, core, near, move(near, to_next_pair)]
    if direct:
        swapped = swap_groups(query_grad)
        input_grad = input_pass(at, query_grad, swapped, pieces)
    else:
        input_grad = input_by_gather(query_grad, query_weight)
    key_grad, value_grad = key_pass(
        at, lists, key_rows, value_rows, queries, out_grad, qg_pairs, stats
    )
    return (input_grad, key_grad, value_grad)


def solution(mesh):
    placed = (
        P("seq", "head"),
        P("seq", "head"),
        P("seq", "head"),
        P("seq", "head"),
        P("seq", "head"),
        P(),
        P(),
    )
    return jax.shard_map(
        gradients,
        mesh=mesh,
        in_specs=placed,
        out_specs=(P("seq", "head"), P("seq", "head"), P("seq", "head")),
        check_vma=False,
    )
```

profile of v0, /device:TPU:4, one launch (start us, length us, event | category | flops | bytes accessed | tf_op | source)
XLA Modules:
  0.0 95.9 jit_solution(15322134163261130910)
XLA Ops:
  0.6 2.7 %collective-permute-start.7 = (bf16[320,384]{1,0:T(8,128)(2,1)}, bf16[320,384]{1,0:T(8,128)(2,1)S(1)}, u32[]{:S(2)}, u32[]{:S(2)}) collective-permute-start(bf16[320,384]{1,0:T(8,128)(2,1)} %param.11), channel_id=1, source_target_pairs={{0,16},{2,18},{4,20},{6,22},{8,24},{10,26},{12,28},{14,30},{16,0},... | collective-permute-start | bytes 737288 | tf_op jit(solution)/shard_map/ppermute | solution.py:22
  3.3 0.7 collective-permute-start.8
  4.0 11.9 %collective-permute-done.7 = bf16[320,384]{1,0:T(8,128)(2,1)S(1)} collective-permute-done((bf16[320,384]{1,0:T(8,128)(2,1)}, bf16[320,384]{1,0:T(8,128)(2,1)S(1)}, u32[]{:S(2)}, u32[]{:S(2)}) %collective-permute-start.7) | collective-permute-done | bytes 245792 | tf_op jit(solution)/shard_map/ppermute | solution.py:22
  15.9 1.3 %collective-permute-start.9 = (bf16[320,384]{1,0:T(8,128)(2,1)S(1)}, bf16[320,384]{1,0:T(8,128)(2,1)S(1)}, u32[]{:S(2)}, u32[]{:S(2)}) collective-permute-start(bf16[320,384]{1,0:T(8,128)(2,1)S(1)} %collective-permute-done.7), channel_id=1, source_target_pairs={{8,0},{10,2},{12,4},{14,6},{16,24},{18,26},{20,28},{22,30},{9,1},{... | collective-permute-start | bytes 737288 | tf_op jit(solution)/shard_map/ppermute | solution.py:22
  17.2 2.7 %collective-permute-start.6 = (bf16[320,384]{1,0:T(8,128)(2,1)}, bf16[320,384]{1,0:T(8,128)(2,1)S(1)}, u32[]{:S(2)}, u32[]{:S(2)}) collective-permute-start(bf16[320,384]{1,0:T(8,128)(2,1)} %param.11), channel_id=1, source_target_pairs={{0,8},{2,10},{4,12},{6,14},{8,0},{10,2},{12,4},{14,6},{16,24},{18,... | collective-permute-start | bytes 737288 | tf_op jit(solution)/shard_map/ppermute | solution.py:22
  19.9 2.2 %pack.1 = (bf16[2,256,384]{2,1,0:T(8,128)(2,1)}, bf16[2,256,384]{2,1,0:T(8,128)(2,1)}, s32[32,128]{1,0:T(8,128)}) custom-call(s32[12,32]{1,0:T(8,128)} %bitcast.11, s32[1,32]{1,0:T(1,128)} %bitcast.12, bf16[256,384]{1,0:T(8,128)(2,1)} %k_ref.5, bf16[256,384]{1,0:T(8,128)(2,1)} %v_ref.5, bf16[256,384]{1,0:T(8,128)(2,1)} %q_ref.5, bf16[256,384]{1,0:T(8,128)(2,1)} %g_ref.5), custom_call_target="tpu_custom_call" | custom-call | tf_op jit(solution)/shard_map/pack/pallas_call | solution.py:235
  22.1 0.2 collective-permute-start.1
  22.3 1.8 %collective-permute-start.18 = (bf16[2,256,384]{2,1,0:T(8,128)(2,1)}, bf16[2,256,384]{2,1,0:T(8,128)(2,1)S(1)}, u32[]{:S(2)}, u32[]{:S(2)}) collective-permute-start(bf16[2,256,384]{2,1,0:T(8,128)(2,1)} %get-tuple-element.13), channel_id=1, source_target_pairs={{0,4},{2,6},{4,0},{6,2},{8,12},{10,14},{12,8},{14,10},{16,20},{18,... | collective-permute-start | bytes 1179656 | tf_op jit(solution)/shard_map/ppermute | solution.py:22
  24.1 0.0 collective-permute-done.8
  24.1 2.1 %collective-permute-done.9 = bf16[320,384]{1,0:T(8,128)(2,1)S(1)} collective-permute-done((bf16[320,384]{1,0:T(8,128)(2,1)S(1)}, bf16[320,384]{1,0:T(8,128)(2,1)S(1)}, u32[]{:S(2)}, u32[]{:S(2)}) %collective-permute-start.9) | collective-permute-done | bytes 245792 | tf_op jit(solution)/shard_map/ppermute | solution.py:22
  26.2 2.6 %collective-permute-done.6 = bf16[320,384]{1,0:T(8,128)(2,1)S(1)} collective-permute-done((bf16[320,384]{1,0:T(8,128)(2,1)}, bf16[320,384]{1,0:T(8,128)(2,1)S(1)}, u32[]{:S(2)}, u32[]{:S(2)}) %collective-permute-start.6) | collective-permute-done | bytes 245792 | tf_op jit(solution)/shard_map/ppermute | solution.py:22
  28.8 0.1 broadcast_select_fusion
  28.9 1.6 %collective-permute-start.13 = (bf16[2,320,384]{2,1,0:T(8,128)(2,1)S(1)}, bf16[2,320,384]{2,1,0:T(8,128)(2,1)S(1)}, u32[]{:S(2)}, u32[]{:S(2)}) collective-permute-start(bf16[2,320,384]{2,1,0:T(8,128)(2,1)S(1)} %get-tuple-element.17), channel_id=1, source_target_pairs={{0,1},{1,0},{2,3},{3,2},{4,5},{5,4},{6,7},{7,6},{8,9},{9,8},{10,11... | collective-permute-start | bytes 1474568 | tf_op jit(solution)/shard_map/ppermute | solution.py:26
  30.5 3.8 %collective-permute-done.1.b2 = bf16[2,256,384]{2,1,0:T(8,128)(2,1)S(1)} collective-permute-done((bf16[2,256,384]{2,1,0:T(8,128)(2,1)}, bf16[2,256,384]{2,1,0:T(8,128)(2,1)S(1)}, u32[]{:S(2)}, u32[]{:S(2)}) %collective-permute-start.1) | collective-permute-done | bytes 393248 | tf_op jit(solution)/shard_map/ppermute | solution.py:22
  34.3 1.3 %collective-permute-start.3 = (bf16[2,256,384]{2,1,0:T(8,128)(2,1)S(1)}, bf16[2,256,384]{2,1,0:T(8,128)(2,1)S(1)}, u32[]{:S(2)}, u32[]{:S(2)}) collective-permute-start(bf16[2,256,384]{2,1,0:T(8,128)(2,1)S(1)} %collective-permute-done.1.b2), channel_id=1, source_target_pairs={{0,8},{2,10},{8,16},{10,18},{12,4},{14,6},{16,24},{18,26},{20,12},... | collective-permute-start | bytes 1179656 | tf_op jit(solution)/shard_map/ppermute | solution.py:22
  35.6 0.1 collective-permute-start
  35.6 0.5 collective-permute-start.2
  36.1 2.9 %collective-permute-done.18.b2 = bf16[2,256,384]{2,1,0:T(8,128)(2,1)S(1)} collective-permute-done((bf16[2,256,384]{2,1,0:T(8,128)(2,1)}, bf16[2,256,384]{2,1,0:T(8,128)(2,1)S(1)}, u32[]{:S(2)}, u32[]{:S(2)}) %collective-permute-start.18) | collective-permute-done | bytes 393248 | tf_op jit(solution)/shard_map/ppermute | solution.py:22
  39.0 1.3 %collective-permute-start.20 = (bf16[2,256,384]{2,1,0:T(8,128)(2,1)S(1)}, bf16[2,256,384]{2,1,0:T(8,128)(2,1)}, u32[]{:S(2)}, u32[]{:S(2)}) collective-permute-start(bf16[2,256,384]{2,1,0:T(8,128)(2,1)S(1)} %collective-permute-done.18.b2), channel_id=1, source_target_pairs={{0,8},{2,10},{8,16},{10,18},{12,4},{14,6},{16,24},{18,26},{20,12},... | collective-permute-start | bytes 1179656 | tf_op jit(solution)/shard_map/ppermute | solution.py:22
  40.3 5.9 %collective-permute-done.3.b4 = bf16[2,256,384]{2,1,0:T(8,128)(2,1)S(1)} collective-permute-done((bf16[2,256,384]{2,1,0:T(8,128)(2,1)S(1)}, bf16[2,256,384]{2,1,0:T(8,128)(2,1)S(1)}, u32[]{:S(2)}, u32[]{:S(2)}) %collective-permute-start.3) | collective-permute-done | bytes 393248 | tf_op jit(solution)/shard_map/ppermute | solution.py:22
  46.2 0.0 collective-permute-start.4
  46.2 0.0 collective-permute-done.b1
  46.2 0.0 copy-start.12
  46.2 0.9 copy-done.12
  47.1 0.0 collective-permute-start.11
  47.1 0.0 collective-permute-done.13.refs_4_
  47.1 2.0 %collective-permute-start.15 = (bf16[2,320,384]{2,1,0:T(8,128)(2,1)S(1)}, bf16[2,320,384]{2,1,0:T(8,128)(2,1)S(1)}, u32[]{:S(2)}, u32[]{:S(2)}) collective-permute-start(bf16[2,320,384]{2,1,0:T(8,128)(2,1)S(1)} %collective-permute-done.13.refs_4_), channel_id=1, source_target_pairs={{0,4},{2,6},{4,0},{6,2},{8,12},{10,14},{12,8},{14,10},{16,20},{18,... | collective-permute-start | bytes 1474568 | tf_op jit(solution)/shard_map/ppermute | solution.py:22
  49.1 0.0 collective-permute-done.2.b3
  49.1 0.0 collective-permute-start.17
  49.1 3.3 %collective-permute-done.20.b4 = bf16[2,256,384]{2,1,0:T(8,128)(2,1)} collective-permute-done((bf16[2,256,384]{2,1,0:T(8,128)(2,1)S(1)}, bf16[2,256,384]{2,1,0:T(8,128)(2,1)}, u32[]{:S(2)}, u32[]{:S(2)}) %collective-permute-start.20) | collective-permute-done | bytes 393248 | tf_op jit(solution)/shard_map/ppermute | solution.py:22
  52.4 0.0 collective-permute-start.19
  52.4 0.0 collective-permute-done.4.b5
  52.5 0.6 collective-permute-start.21
  53.0 0.2 copy-done.14
  53.2 5.8 %query_pass.1 = (bf16[256,384]{1,0:T(8,128)(2,1)}, f32[8,256]{1,0:T(8,128)}) custom-call(s32[1]{0:T(128)} %bitcast.at_ref, s32[32,128]{1,0:T(8,128)} %get-tuple-element.10.lists_ref, bf16[256,384]{1,0:T(8,128)(2,1)} %q_ref.5, bf16[256,384]{1,0:T(8,128)(2,1)} %g_ref.5, bf16[256,384]{1,0:T(8,128)(2,1)} %k_ref.5, bf16[256,384]{1,0:T(8,128)(2,1)} %v_ref.5, ...), custom_call_target="tpu_custom_call" | custom-call | tf_op jit(solution)/shard_map/query_pass/pallas_call | solution.py:188
  59.0 0.0 collective-permute-done.17.b1
  59.0 0.0 copy-start.9
  59.0 0.6 collective-permute-start.22
  59.6 0.0 collective-permute-done.19.b3
  59.6 0.1 collective-permute-start.10
  59.7 0.1 copy-done.9
  59.8 1.4 %collective-permute-done.11.refs_2_ = bf16[2,320,384]{2,1,0:T(8,128)(2,1)S(1)} collective-permute-done((bf16[2,320,384]{2,1,0:T(8,128)(2,1)S(1)}, bf16[2,320,384]{2,1,0:T(8,128)(2,1)S(1)}, u32[]{:S(2)}, u32[]{:S(2)}) %collective-permute-start.11) | collective-permute-done | bytes 491552 | tf_op jit(solution)/shard_map/ppermute | solution.py:22
  61.2 0.0 collective-permute-start.14
  61.2 0.0 collective-permute-done.22.t1
  61.2 0.5 collective-permute-start.12
  61.8 9.4 %collective-permute-done.15.refs_6_ = bf16[2,320,384]{2,1,0:T(8,128)(2,1)S(1)} collective-permute-done((bf16[2,320,384]{2,1,0:T(8,128)(2,1)S(1)}, bf16[2,320,384]{2,1,0:T(8,128)(2,1)S(1)}, u32[]{:S(2)}, u32[]{:S(2)}) %collective-permute-start.15) | collective-permute-done | bytes 491552 | tf_op jit(solution)/shard_map/ppermute | solution.py:22
  71.1 0.0 collective-permute-start.16
  71.1 0.7 pad_maximum_fusion.2
  71.8 0.0 collective-permute-done.21.b5
  71.9 0.3 collective-permute-start.23
  72.1 3.5 %collective-permute-done.23.t2 = f32[16,256]{1,0:T(8,128)S(1)} collective-permute-done((f32[16,256]{1,0:T(8,128)S(1)}, f32[16,256]{1,0:T(8,128)S(1)}, u32[]{:S(2)}, u32[]{:S(2)}) %collective-permute-start.23) | collective-permute-done | bytes 16416 | tf_op jit(solution)/shard_map/ppermute | solution.py:22
  75.6 1.3 %collective-permute-start.24 = (f32[16,256]{1,0:T(8,128)S(1)}, f32[16,256]{1,0:T(8,128)S(1)}, u32[]{:S(2)}, u32[]{:S(2)}) collective-permute-start(f32[16,256]{1,0:T(8,128)S(1)} %collective-permute-done.23.t2), channel_id=1, source_target_pairs={{0,8},{2,10},{8,16},{10,18},{12,4},{14,6},{16,24},{18,26},{20,12},... | collective-permute-start | bytes 49160 | tf_op jit(solution)/shard_map/ppermute | solution.py:22
  76.9 4.3 %collective-permute-done.24.t4 = f32[16,256]{1,0:T(8,128)S(1)} collective-permute-done((f32[16,256]{1,0:T(8,128)S(1)}, f32[16,256]{1,0:T(8,128)S(1)}, u32[]{:S(2)}, u32[]{:S(2)}) %collective-permute-start.24) | collective-permute-done | bytes 16416 | tf_op jit(solution)/shard_map/ppermute | solution.py:22
  81.2 1.5 %collective-permute-start.5 = (bf16[256,384]{1,0:T(8,128)(2,1)}, bf16[256,384]{1,0:T(8,128)(2,1)}, u32[]{:S(2)}, u32[]{:S(2)}) collective-permute-start(bf16[256,384]{1,0:T(8,128)(2,1)} %get-tuple-element.12.own_ref), channel_id=1, source_target_pairs={{0,1},{1,0},{2,3},{3,2},{4,5},{5,4},{6,7},{7,6},{8,9},{9,8},{10,11... | collective-permute-start | bytes 589832 | tf_op jit(solution)/shard_map/ppermute | solution.py:26
  82.7 6.4 %key_pass.1 = (bf16[256,384]{1,0:T(8,128)(2,1)}, bf16[256,384]{1,0:T(8,128)(2,1)}) custom-call(s32[1]{0:T(128)} %bitcast.at_ref, s32[32,128]{1,0:T(8,128)} %get-tuple-element.10.lists_ref, bf16[256,384]{1,0:T(8,128)(2,1)} %k_ref.5, bf16[256,384]{1,0:T(8,128)(2,1)} %v_ref.5, bf16[256,384]{1,0:T(8,128)(2,1)} %q_ref.5, bf16[256,384]{1,0:T(8,128)(2,1)} %g_ref.5, ...), custom_call_target="tpu_custom_call" | custom-call | tf_op jit(solution)/shard_map/key_pass/pallas_call | solution.py:204
  89.1 0.0 collective-permute-done.10.refs_1_
  89.2 0.0 collective-permute-done.5.other_ref
  89.2 0.0 collective-permute-done.12.refs_3_
  89.2 0.0 collective-permute-done.14.refs_5_
  89.2 0.0 collective-permute-done.16.refs_7_
  89.2 0.7 copy-done.4
  89.9 0.2 copy-done.6
  90.1 0.2 copy-done.5
  90.3 5.7 %input_pass.1 = bf16[256,2560]{1,0:T(8,128)(2,1)} custom-call(s32[1]{0:T(128)} %bitcast.at_ref, bf16[256,384]{1,0:T(8,128)(2,1)} %get-tuple-element.12.own_ref, bf16[256,384]{1,0:T(8,128)(2,1)} %collective-permute-done.5.other_ref, bf16[2,320,384]{2,1,0:T(8,128)(2,1)} %copy-done, bf16[2,320,384]{2,1,0:T(8,128)(2,1)} %copy-done.4, ...), custom_call_target="tpu_custom_call" | custom-call | tf_op jit(solution)/shard_map/input_pass/pallas_call | solution.py:288
  (33 shorter events, 0.1 us)
Async XLA Ops:
  0.6 28.2 %copy-start.15 = (bf16[320,384]{1,0:T(8,128)(2,1)S(1)}, bf16[320,384]{1,0:T(8,128)(2,1)}, u32[]{:S(2)}) copy-start(bf16[320,384]{1,0:T(8,128)(2,1)} %param.11) | copy-start | bytes 737284
  0.6 15.2 %collective-permute-start.7 = (bf16[320,384]{1,0:T(8,128)(2,1)}, bf16[320,384]{1,0:T(8,128)(2,1)S(1)}, u32[]{:S(2)}, u32[]{:S(2)}) collective-permute-start(bf16[320,384]{1,0:T(8,128)(2,1)} %param.11), channel_id=1, source_target_pairs={{0,16},{2,18},{4,20},{6,22},{8,24},{10,26},{12,28},{14,30},{16,0},... | collective-permute-start | bytes 737288 | tf_op jit(solution)/shard_map/ppermute | solution.py:22
  3.3 20.8 %collective-permute-start.8 = (bf16[320,384]{1,0:T(8,128)(2,1)}, bf16[320,384]{1,0:T(8,128)(2,1)S(1)}, u32[]{:S(2)}, u32[]{:S(2)}) collective-permute-start(bf16[320,384]{1,0:T(8,128)(2,1)} %param.11), channel_id=1, source_target_pairs={{8,16},{10,18},{12,20},{14,22},{16,8},{18,10},{20,12},{22,14},{9,1... | collective-permute-start | bytes 737288 | tf_op jit(solution)/shard_map/ppermute | solution.py:22
  15.9 10.3 %collective-permute-start.9 = (bf16[320,384]{1,0:T(8,128)(2,1)S(1)}, bf16[320,384]{1,0:T(8,128)(2,1)S(1)}, u32[]{:S(2)}, u32[]{:S(2)}) collective-permute-start(bf16[320,384]{1,0:T(8,128)(2,1)S(1)} %collective-permute-done.7), channel_id=1, source_target_pairs={{8,0},{10,2},{12,4},{14,6},{16,24},{18,26},{20,28},{22,30},{9,1},{... | collective-permute-start | bytes 737288 | tf_op jit(solution)/shard_map/ppermute | solution.py:22
  17.2 11.6 %collective-permute-start.6 = (bf16[320,384]{1,0:T(8,128)(2,1)}, bf16[320,384]{1,0:T(8,128)(2,1)S(1)}, u32[]{:S(2)}, u32[]{:S(2)}) collective-permute-start(bf16[320,384]{1,0:T(8,128)(2,1)} %param.11), channel_id=1, source_target_pairs={{0,8},{2,10},{4,12},{6,14},{8,0},{10,2},{12,4},{14,6},{16,24},{18,... | collective-permute-start | bytes 737288 | tf_op jit(solution)/shard_map/ppermute | solution.py:22
  22.1 12.2 %collective-permute-start.1 = (bf16[2,256,384]{2,1,0:T(8,128)(2,1)}, bf16[2,256,384]{2,1,0:T(8,128)(2,1)S(1)}, u32[]{:S(2)}, u32[]{:S(2)}) collective-permute-start(bf16[2,256,384]{2,1,0:T(8,128)(2,1)} %get-tuple-element.11), channel_id=1, source_target_pairs={{0,4},{2,6},{4,0},{6,2},{8,12},{10,14},{12,8},{14,10},{16,20},{18,... | collective-permute-start | bytes 1179656 | tf_op jit(solution)/shard_map/ppermute | solution.py:22
  22.3 16.8 %collective-permute-start.18 = (bf16[2,256,384]{2,1,0:T(8,128)(2,1)}, bf16[2,256,384]{2,1,0:T(8,128)(2,1)S(1)}, u32[]{:S(2)}, u32[]{:S(2)}) collective-permute-start(bf16[2,256,384]{2,1,0:T(8,128)(2,1)} %get-tuple-element.13), channel_id=1, source_target_pairs={{0,4},{2,6},{4,0},{6,2},{8,12},{10,14},{12,8},{14,10},{16,20},{18,... | collective-permute-start | bytes 1179656 | tf_op jit(solution)/shard_map/ppermute | solution.py:22
  24.1 11.5 %copy-start.19 = (bf16[2,256,384]{2,1,0:T(8,128)(2,1)S(1)}, bf16[2,256,384]{2,1,0:T(8,128)(2,1)}, u32[]{:S(2)}) copy-start(bf16[2,256,384]{2,1,0:T(8,128)(2,1)} %get-tuple-element.11) | copy-start | bytes 1179652
  28.9 30.7 %copy-start = (bf16[2,320,384]{2,1,0:T(8,128)(2,1)}, bf16[2,320,384]{2,1,0:T(8,128)(2,1)S(1)}, u32[]{:S(2)}) copy-start(bf16[2,320,384]{2,1,0:T(8,128)(2,1)S(1)} %get-tuple-element.18.refs_0_) | copy-start | bytes 1474564
  28.9 18.2 %collective-permute-start.13 = (bf16[2,320,384]{2,1,0:T(8,128)(2,1)S(1)}, bf16[2,320,384]{2,1,0:T(8,128)(2,1)S(1)}, u32[]{:S(2)}, u32[]{:S(2)}) collective-permute-start(bf16[2,320,384]{2,1,0:T(8,128)(2,1)S(1)} %get-tuple-element.17), channel_id=1, source_target_pairs={{0,1},{1,0},{2,3},{3,2},{4,5},{5,4},{6,7},{7,6},{8,9},{9,8},{10,11... | collective-permute-start | bytes 1474568 | tf_op jit(solution)/shard_map/ppermute | solution.py:26
  34.2 19.0 %copy-start.8 = (bf16[2,256,384]{2,1,0:T(8,128)(2,1)}, bf16[2,256,384]{2,1,0:T(8,128)(2,1)S(1)}, u32[]{:S(2)}) copy-start(bf16[2,256,384]{2,1,0:T(8,128)(2,1)S(1)} %collective-permute-done.1.b2) | copy-start | bytes 1179652
  34.3 12.0 %collective-permute-start.3 = (bf16[2,256,384]{2,1,0:T(8,128)(2,1)S(1)}, bf16[2,256,384]{2,1,0:T(8,128)(2,1)S(1)}, u32[]{:S(2)}, u32[]{:S(2)}) collective-permute-start(bf16[2,256,384]{2,1,0:T(8,128)(2,1)S(1)} %collective-permute-done.1.b2), channel_id=1, source_target_pairs={{0,8},{2,10},{8,16},{10,18},{12,4},{14,6},{16,24},{18,26},{20,12},... | collective-permute-start | bytes 1179656 | tf_op jit(solution)/shard_map/ppermute | solution.py:22
  35.6 10.7 %collective-permute-start = (bf16[2,256,384]{2,1,0:T(8,128)(2,1)S(1)}, bf16[2,256,384]{2,1,0:T(8,128)(2,1)S(1)}, u32[]{:S(2)}, u32[]{:S(2)}) collective-permute-start(bf16[2,256,384]{2,1,0:T(8,128)(2,1)S(1)} %copy-done.19), channel_id=1, source_target_pairs={{0,2},{2,0},{4,6},{6,4},{8,10},{10,8},{12,14},{14,12},{16,18},{18,... | collective-permute-start | bytes 1179656 | tf_op jit(solution)/shard_map/ppermute | solution.py:22
  35.6 13.5 %collective-permute-start.2 = (bf16[2,256,384]{2,1,0:T(8,128)(2,1)S(1)}, bf16[2,256,384]{2,1,0:T(8,128)(2,1)S(1)}, u32[]{:S(2)}, u32[]{:S(2)}) collective-permute-start(bf16[2,256,384]{2,1,0:T(8,128)(2,1)S(1)} %collective-permute-done.1.b2), channel_id=1, source_target_pairs={{0,2},{2,0},{4,6},{6,4},{8,10},{10,8},{12,14},{14,12},{16,18},{18,... | collective-permute-start | bytes 1179656 | tf_op jit(solution)/shard_map/ppermute | solution.py:22
  39.0 20.0 %copy-start.7 = (bf16[2,256,384]{2,1,0:T(8,128)(2,1)}, bf16[2,256,384]{2,1,0:T(8,128)(2,1)S(1)}, u32[]{:S(2)}) copy-start(bf16[2,256,384]{2,1,0:T(8,128)(2,1)S(1)} %collective-permute-done.18.b2) | copy-start | bytes 1179652
  39.0 13.4 %collective-permute-start.20 = (bf16[2,256,384]{2,1,0:T(8,128)(2,1)S(1)}, bf16[2,256,384]{2,1,0:T(8,128)(2,1)}, u32[]{:S(2)}, u32[]{:S(2)}) collective-permute-start(bf16[2,256,384]{2,1,0:T(8,128)(2,1)S(1)} %collective-permute-done.18.b2), channel_id=1, source_target_pairs={{0,8},{2,10},{8,16},{10,18},{12,4},{14,6},{16,24},{18,26},{20,12},... | collective-permute-start | bytes 1179656 | tf_op jit(solution)/shard_map/ppermute | solution.py:22
  46.2 6.2 %copy-start.11 = (bf16[2,256,384]{2,1,0:T(8,128)(2,1)}, bf16[2,256,384]{2,1,0:T(8,128)(2,1)S(1)}, u32[]{:S(2)}) copy-start(bf16[2,256,384]{2,1,0:T(8,128)(2,1)S(1)} %collective-permute-done.3.b4) | copy-start | bytes 1179652
  46.2 6.2 %collective-permute-start.4 = (bf16[2,256,384]{2,1,0:T(8,128)(2,1)S(1)}, bf16[2,256,384]{2,1,0:T(8,128)(2,1)S(1)}, u32[]{:S(2)}, u32[]{:S(2)}) collective-permute-start(bf16[2,256,384]{2,1,0:T(8,128)(2,1)S(1)} %collective-permute-done.3.b4), channel_id=1, source_target_pairs={{0,2},{2,0},{4,6},{6,4},{8,10},{10,8},{12,14},{14,12},{16,18},{18,... | collective-permute-start | bytes 1179656 | tf_op jit(solution)/shard_map/ppermute | solution.py:22
  46.2 0.9 copy-start.12
  47.1 14.1 %collective-permute-start.11 = (bf16[2,320,384]{2,1,0:T(8,128)(2,1)S(1)}, bf16[2,320,384]{2,1,0:T(8,128)(2,1)S(1)}, u32[]{:S(2)}, u32[]{:S(2)}) collective-permute-start(bf16[2,320,384]{2,1,0:T(8,128)(2,1)S(1)} %get-tuple-element.18.refs_0_), channel_id=1, source_target_pairs={{0,4},{2,6},{4,0},{6,2},{8,12},{10,14},{12,8},{14,10},{16,20},{18,... | collective-permute-start | bytes 1474568 | tf_op jit(solution)/shard_map/ppermute | solution.py:22
  47.1 14.1 %copy-start.1 = (bf16[2,320,384]{2,1,0:T(8,128)(2,1)}, bf16[2,320,384]{2,1,0:T(8,128)(2,1)S(1)}, u32[]{:S(2)}) copy-start(bf16[2,320,384]{2,1,0:T(8,128)(2,1)S(1)} %collective-permute-done.13.refs_4_) | copy-start | bytes 1474564
  47.1 24.0 %collective-permute-start.15 = (bf16[2,320,384]{2,1,0:T(8,128)(2,1)S(1)}, bf16[2,320,384]{2,1,0:T(8,128)(2,1)S(1)}, u32[]{:S(2)}, u32[]{:S(2)}) collective-permute-start(bf16[2,320,384]{2,1,0:T(8,128)(2,1)S(1)} %collective-permute-done.13.refs_4_), channel_id=1, source_target_pairs={{0,4},{2,6},{4,0},{6,2},{8,12},{10,14},{12,8},{14,10},{16,20},{18,... | collective-permute-start | bytes 1474568 | tf_op jit(solution)/shard_map/ppermute | solution.py:22
  49.1 3.3 %copy-start.13 = (bf16[2,256,384]{2,1,0:T(8,128)(2,1)}, bf16[2,256,384]{2,1,0:T(8,128)(2,1)S(1)}, u32[]{:S(2)}) copy-start(bf16[2,256,384]{2,1,0:T(8,128)(2,1)S(1)} %collective-permute-done.2.b3) | copy-start | bytes 1179652
  49.1 9.9 %collective-permute-start.17 = (bf16[2,256,384]{2,1,0:T(8,128)(2,1)}, bf16[2,256,384]{2,1,0:T(8,128)(2,1)S(1)}, u32[]{:S(2)}, u32[]{:S(2)}) collective-permute-start(bf16[2,256,384]{2,1,0:T(8,128)(2,1)} %get-tuple-element.13), channel_id=1, source_target_pairs={{0,2},{2,0},{4,6},{6,4},{8,10},{10,8},{12,14},{14,12},{16,18},{18,... | collective-permute-start | bytes 1179656 | tf_op jit(solution)/shard_map/ppermute | solution.py:22
  52.4 7.2 %collective-permute-start.19 = (bf16[2,256,384]{2,1,0:T(8,128)(2,1)S(1)}, bf16[2,256,384]{2,1,0:T(8,128)(2,1)S(1)}, u32[]{:S(2)}, u32[]{:S(2)}) collective-permute-start(bf16[2,256,384]{2,1,0:T(8,128)(2,1)S(1)} %collective-permute-done.18.b2), channel_id=1, source_target_pairs={{0,2},{2,0},{4,6},{6,4},{8,10},{10,8},{12,14},{14,12},{16,18},{18,... | collective-permute-start | bytes 1179656 | tf_op jit(solution)/shard_map/ppermute | solution.py:22
  52.5 0.8 copy-start.14
  52.5 19.4 %collective-permute-start.21 = (bf16[2,256,384]{2,1,0:T(8,128)(2,1)}, bf16[2,256,384]{2,1,0:T(8,128)(2,1)}, u32[]{:S(2)}, u32[]{:S(2)}) collective-permute-start(bf16[2,256,384]{2,1,0:T(8,128)(2,1)} %collective-permute-done.20.b4), channel_id=1, source_target_pairs={{0,2},{2,0},{4,6},{6,4},{8,10},{10,8},{12,14},{14,12},{16,18},{18,... | collective-permute-start | bytes 1179656 | tf_op jit(solution)/shard_map/ppermute | solution.py:22
  59.0 0.7 copy-start.9
  59.0 2.2 %collective-permute-start.22 = (f32[8,256]{1,0:T(8,128)}, f32[8,256]{1,0:T(8,128)S(1)}, u32[]{:S(2)}, u32[]{:S(2)}) collective-permute-start(f32[8,256]{1,0:T(8,128)} %get-tuple-element.14.t0), channel_id=1, source_target_pairs={{0,2},{2,0},{4,6},{6,4},{8,10},{10,8},{12,14},{14,12},{16,18},{18,... | collective-permute-start | bytes 24584 | tf_op jit(solution)/shard_map/ppermute | solution.py:22
  59.6 1.6 %copy-start.10 = (bf16[2,256,384]{2,1,0:T(8,128)(2,1)}, bf16[2,256,384]{2,1,0:T(8,128)(2,1)S(1)}, u32[]{:S(2)}) copy-start(bf16[2,256,384]{2,1,0:T(8,128)(2,1)S(1)} %collective-permute-done.19.b3) | copy-start | bytes 1179652
  59.6 29.5 %collective-permute-start.10 = (bf16[2,320,384]{2,1,0:T(8,128)(2,1)S(1)}, bf16[2,320,384]{2,1,0:T(8,128)(2,1)S(1)}, u32[]{:S(2)}, u32[]{:S(2)}) collective-permute-start(bf16[2,320,384]{2,1,0:T(8,128)(2,1)S(1)} %get-tuple-element.18.refs_0_), channel_id=1, source_target_pairs={{0,2},{2,0},{4,6},{6,4},{8,10},{10,8},{12,14},{14,12},{16,18},{18,... | collective-permute-start | bytes 1474568 | tf_op jit(solution)/shard_map/ppermute | solution.py:22
  61.2 27.9 %copy-start.2 = (bf16[2,320,384]{2,1,0:T(8,128)(2,1)}, bf16[2,320,384]{2,1,0:T(8,128)(2,1)S(1)}, u32[]{:S(2)}) copy-start(bf16[2,320,384]{2,1,0:T(8,128)(2,1)S(1)} %collective-permute-done.11.refs_2_) | copy-start | bytes 1474564
  61.2 28.0 %collective-permute-start.14 = (bf16[2,320,384]{2,1,0:T(8,128)(2,1)S(1)}, bf16[2,320,384]{2,1,0:T(8,128)(2,1)S(1)}, u32[]{:S(2)}, u32[]{:S(2)}) collective-permute-start(bf16[2,320,384]{2,1,0:T(8,128)(2,1)S(1)} %collective-permute-done.13.refs_4_), channel_id=1, source_target_pairs={{0,2},{2,0},{4,6},{6,4},{8,10},{10,8},{12,14},{14,12},{16,18},{18,... | collective-permute-start | bytes 1474568 | tf_op jit(solution)/shard_map/ppermute | solution.py:22
  61.2 21.5 %copy-start.16 = (f32[8,256]{1,0:T(8,128)}, f32[8,256]{1,0:T(8,128)S(1)}, u32[]{:S(2)}) copy-start(f32[8,256]{1,0:T(8,128)S(1)} %collective-permute-done.22.t1) | copy-start | bytes 24580
  61.2 27.9 %collective-permute-start.12 = (bf16[2,320,384]{2,1,0:T(8,128)(2,1)S(1)}, bf16[2,320,384]{2,1,0:T(8,128)(2,1)S(1)}, u32[]{:S(2)}, u32[]{:S(2)}) collective-permute-start(bf16[2,320,384]{2,1,0:T(8,128)(2,1)S(1)} %collective-permute-done.11.refs_2_), channel_id=1, source_target_pairs={{0,2},{2,0},{4,6},{6,4},{8,10},{10,8},{12,14},{14,12},{16,18},{18,... | collective-permute-start | bytes 1474568 | tf_op jit(solution)/shard_map/ppermute | solution.py:22
  71.1 18.0 %copy-start.3 = (bf16[2,320,384]{2,1,0:T(8,128)(2,1)}, bf16[2,320,384]{2,1,0:T(8,128)(2,1)S(1)}, u32[]{:S(2)}) copy-start(bf16[2,320,384]{2,1,0:T(8,128)(2,1)S(1)} %collective-permute-done.15.refs_6_) | copy-start | bytes 1474564
  71.1 18.1 %collective-permute-start.16 = (bf16[2,320,384]{2,1,0:T(8,128)(2,1)S(1)}, bf16[2,320,384]{2,1,0:T(8,128)(2,1)}, u32[]{:S(2)}, u32[]{:S(2)}) collective-permute-start(bf16[2,320,384]{2,1,0:T(8,128)(2,1)S(1)} %collective-permute-done.15.refs_6_), channel_id=1, source_target_pairs={{0,2},{2,0},{4,6},{6,4},{8,10},{10,8},{12,14},{14,12},{16,18},{18,... | collective-permute-start | bytes 1474568 | tf_op jit(solution)/shard_map/ppermute | solution.py:22
  71.9 3.7 %collective-permute-start.23 = (f32[16,256]{1,0:T(8,128)S(1)}, f32[16,256]{1,0:T(8,128)S(1)}, u32[]{:S(2)}, u32[]{:S(2)}) collective-permute-start(f32[16,256]{1,0:T(8,128)S(1)} %pad_maximum_fusion.2), channel_id=1, source_target_pairs={{0,4},{2,6},{4,0},{6,2},{8,12},{10,14},{12,8},{14,10},{16,20},{18,... | collective-permute-start | bytes 49160 | tf_op jit(solution)/shard_map/ppermute | solution.py:22
  75.6 7.1 %copy-start.17 = (f32[16,256]{1,0:T(8,128)}, f32[16,256]{1,0:T(8,128)S(1)}, u32[]{:S(2)}) copy-start(f32[16,256]{1,0:T(8,128)S(1)} %collective-permute-done.23.t2) | copy-start | bytes 49156
  75.6 5.6 %collective-permute-start.24 = (f32[16,256]{1,0:T(8,128)S(1)}, f32[16,256]{1,0:T(8,128)S(1)}, u32[]{:S(2)}, u32[]{:S(2)}) collective-permute-start(f32[16,256]{1,0:T(8,128)S(1)} %collective-permute-done.23.t2), channel_id=1, source_target_pairs={{0,8},{2,10},{8,16},{10,18},{12,4},{14,6},{16,24},{18,26},{20,12},... | collective-permute-start | bytes 49160 | tf_op jit(solution)/shard_map/ppermute | solution.py:22
  81.2 1.5 %copy-start.18 = (f32[16,256]{1,0:T(8,128)}, f32[16,256]{1,0:T(8,128)S(1)}, u32[]{:S(2)}) copy-start(f32[16,256]{1,0:T(8,128)S(1)} %collective-permute-done.24.t4) | copy-start | bytes 49156
  81.2 7.9 %collective-permute-start.5 = (bf16[256,384]{1,0:T(8,128)(2,1)}, bf16[256,384]{1,0:T(8,128)(2,1)}, u32[]{:S(2)}, u32[]{:S(2)}) collective-permute-start(bf16[256,384]{1,0:T(8,128)(2,1)} %get-tuple-element.12.own_ref), channel_id=1, source_target_pairs={{0,1},{1,0},{2,3},{3,2},{4,5},{5,4},{6,7},{7,6},{8,9},{9,8},{10,11... | collective-permute-start | bytes 589832 | tf_op jit(solution)/shard_map/ppermute | solution.py:26
  89.2 0.8 copy-start.4
  89.2 0.9 copy-start.6
  89.2 1.1 %copy-start.5 = (bf16[2,320,384]{2,1,0:T(8,128)(2,1)}, bf16[2,320,384]{2,1,0:T(8,128)(2,1)S(1)}, u32[]{:S(2)}) copy-start(bf16[2,320,384]{2,1,0:T(8,128)(2,1)S(1)} %collective-permute-done.14.refs_5_) | copy-start | bytes 1474564
where the time goes:
time: 96.3 us; the launch traced here: 95.9 us
  waiting for transfers between devices  51.1 us (53%)
  starting transfers between devices  20.9 us (22%)
  Pallas kernels  20 us (21%)
  local copies, waits for them, and re-layouts  2.24 us (2%)
    ppermute x23, waiting for transfers between devices, move(): lax.ppermute(block, 'seq', [(i, j) for i, j in pairs if 0 <= j < size])  51 us
    ppermute x23, starting transfers between devices, move(): lax.ppermute(block, 'seq', [(i, j) for i, j in pairs if 0 <= j < size])  17.8 us
    pallas_call x1, Pallas kernels, key_pass(): pl.pallas_call(key_kernel, in_specs=[SMEM] + [VMEM] * 14, out_specs=[VMEM...  6.41 us
    pallas_call x1, Pallas kernels, query_pass(): pl.pallas_call(query_kernel, in_specs=[SMEM] + [VMEM] * 10, out_specs=[VM...  5.78 us
    pallas_call x1, Pallas kernels, input_pass(): pl.pallas_call(input_kernel, in_specs=[SMEM, VMEM, VMEM] + [ANYWHERE] * 8...  5.66 us
    ppermute x2, starting transfers between devices, swap_groups(): return lax.ppermute(block, 'head', [(0, 1), (1, 0)])  3.05 us
    unnamed x40, local copies, waits for them, and re-layouts  2.24 us
    pallas_call x1, Pallas kernels, pack(): pl.pallas_call(pack_kernel, in_specs=[VMEM] * 6, out_specs=[VMEM] * 3, ou...  2.16 us
  transfers between devices with their start and end apart: 25, of which 11 were waited for; matrix products, arithmetic and copies ran while one was open for 1% of the time, Pallas kernels for 15%

commit v1 on v0

--- a/solution.py
+++ b/solution.py
@@ -36,6 +36,10 @@
 
 def to_next_pair(i):
     return i + 4 if i % 4 < 2 else i - 4
+
+
+def to_far_pair(i):
+    return i - 2 if i % 4 < 2 else i + 2
 
 
 def owners(position):
@@ -275,29 +279,35 @@
         copy.wait()
 
 
-def input_kernel(at_ref, own_ref, other_ref, *refs):
-    pieces = refs[:8]
-    out_ref, w_ref, o_ref, sems, out_sems = refs[8:]
+def final_kernel(*refs):
+    at_ref = refs[0]
+    key_args, refs = refs[:15], refs[15:]
+    own_ref, other_ref = refs[:2]
+    pieces, refs = refs[2:10], refs[10:]
+    dk_ref, dv_ref, out_ref, mask_ref, w_ref, o_ref, sems, out_sems = refs
     copies = start_input(at_ref, pieces, w_ref, sems)
+    key_kernel(*key_args, dk_ref, dv_ref, mask_ref)
     finish_input(at_ref, own_ref, other_ref, copies, w_ref, o_ref, out_ref, out_sems)
 
 
-def input_pass(at, own, other, pieces):
-    rows, width = own.shape
+def final_pass(at, lists, keys, values, queries, out_grad, pairs, stats, own, other, pieces):
+    rows, width = queries.shape
     span = pieces[0].shape[1] * 4
     return pl.pallas_call(
-        input_kernel,
-        in_specs=[SMEM, VMEM, VMEM] + [ANYWHERE] * 8,
-        out_specs=ANYWHERE,
-        out_shape=jax.ShapeDtypeStruct((rows, 2 * span), jnp.bfloat16),
+        final_kernel,
+        in_specs=[SMEM] + [VMEM] * 16 + [ANYWHERE] * 8,
+        out_specs=[VMEM, VMEM, ANYWHERE],
+        out_shape=[jax.ShapeDtypeStruct((rows, width), jnp.bfloat16)] * 2
+        + [jax.ShapeDtypeStruct((rows, 2 * span), jnp.bfloat16)],
         scratch_shapes=[
+            pltpu.VMEM((TILES_DEV, lists.shape[0], TILE), jnp.float32),
             pltpu.VMEM((2, 2, span, width), jnp.bfloat16),
             pltpu.VMEM((2, rows, span), jnp.bfloat16),
             pltpu.SemaphoreType.DMA((16,)),
             pltpu.SemaphoreType.DMA((2,)),
         ],
-        name="input_pass",
-    )(at, own, other, *pieces)
+        name="final_pass",
+    )(at, lists, keys, values, queries, out_grad, *pairs, *stats, own, other, *pieces)
 
 
 def spread_weight(weight, position, group):
@@ -361,16 +371,19 @@
         at, lists, queries, out_grad, key_rows, value_rows, kv_pairs
     )
     core = move(own, to_core)
-    near = move(jnp.concatenate([own, core]), to_frame_pair)
-    stats = [own, core, near, move(near, to_next_pair)]
+    both = jnp.concatenate([own, core])
+    stats = [own, core, move(both, to_frame_pair), move(both, to_far_pair)]
     if direct:
         swapped = swap_groups(query_grad)
-        input_grad = input_pass(at, query_grad, swapped, pieces)
+        key_grad, value_grad, input_grad = final_pass(
+            at, lists, key_rows, value_rows, queries, out_grad, qg_pairs, stats,
+            query_grad, swapped, pieces,
+        )
     else:
         input_grad = input_by_gather(query_grad, query_weight)
-    key_grad, value_grad = key_pass(
-        at, lists, key_rows, value_rows, queries, out_grad, qg_pairs, stats
-    )
+        key_grad, value_grad = key_pass(
+            at, lists, key_rows, value_rows, queries, out_grad, qg_pairs, stats
+        )
     return (input_grad, key_grad, value_grad)
 
 

time: 96.3 us -> 97.2 us (level)
  the two profiles are of different devices: /device:TPU:4 before, /device:TPU:8 now
where the time goes in v1:
time: 97.2 us; the launch traced here: 96.9 us
  waiting for transfers between devices  47.3 us (49%)
  starting transfers between devices  28.9 us (30%)
  Pallas kernels  17.5 us (18%)
  local copies, waits for them, and re-layouts  1.96 us (2%)
    ppermute x23, waiting for transfers between devices, move(): lax.ppermute(block, 'seq', [(i, j) for i, j in pairs if 0 <= j < size])  47.3 us
    ppermute x23, starting transfers between devices, move(): lax.ppermute(block, 'seq', [(i, j) for i, j in pairs if 0 <= j < size])  26.1 us
    pallas_call x1, Pallas kernels, final_pass(): pl.pallas_call(final_kernel, in_specs=[SMEM] + [VMEM] * 16 + [ANYWHERE] *...  9.59 us
    pallas_call x1, Pallas kernels, query_pass(): pl.pallas_call(query_kernel, in_specs=[SMEM] + [VMEM] * 10, out_specs=[VM...  5.78 us
    ppermute x2, starting transfers between devices, swap_groups(): return lax.ppermute(block, 'head', [(0, 1), (1, 0)])  2.84 us
    pallas_call x1, Pallas kernels, pack(): pl.pallas_call(pack_kernel, in_specs=[VMEM] * 6, out_specs=[VMEM] * 3, ou...  2.17 us
    unnamed x43, local copies, waits for them, and re-layouts  1.96 us
  transfers between devices with their start and end apart: 25, of which 11 were waited for; matrix products, arithmetic and copies ran while one was open for 1% of the time, Pallas kernels for 8%

profile of v1, /device:TPU:8, one launch (start us, length us, event | category | flops | bytes accessed | tf_op | source)
XLA Modules:
  0.0 96.9 jit_solution(1934304744203995637)
XLA Ops:
  0.6 2.7 %collective-permute-start.15 = (bf16[320,384]{1,0:T(8,128)(2,1)}, bf16[320,384]{1,0:T(8,128)(2,1)S(1)}, u32[]{:S(2)}, u32[]{:S(2)}) collective-permute-start(bf16[320,384]{1,0:T(8,128)(2,1)} %param.11), channel_id=1, source_target_pairs={{0,16},{2,18},{4,20},{6,22},{8,24},{10,26},{12,28},{14,30},{16,0},... | collective-permute-start | bytes 737288 | tf_op jit(solution)/shard_map/ppermute | solution.py:22
  3.3 1.9 %collective-permute-start.16 = (bf16[320,384]{1,0:T(8,128)(2,1)}, bf16[320,384]{1,0:T(8,128)(2,1)S(1)}, u32[]{:S(2)}, u32[]{:S(2)}) collective-permute-start(bf16[320,384]{1,0:T(8,128)(2,1)} %param.11), channel_id=1, source_target_pairs={{8,16},{10,18},{12,20},{14,22},{16,8},{18,10},{20,12},{22,14},{9,1... | collective-permute-start | bytes 737288 | tf_op jit(solution)/shard_map/ppermute | solution.py:22
  5.2 8.9 %collective-permute-done.15 = bf16[320,384]{1,0:T(8,128)(2,1)S(1)} collective-permute-done((bf16[320,384]{1,0:T(8,128)(2,1)}, bf16[320,384]{1,0:T(8,128)(2,1)S(1)}, u32[]{:S(2)}, u32[]{:S(2)}) %collective-permute-start.15) | collective-permute-done | bytes 245792 | tf_op jit(solution)/shard_map/ppermute | solution.py:22
  14.1 3.9 %collective-permute-start.17 = (bf16[320,384]{1,0:T(8,128)(2,1)S(1)}, bf16[320,384]{1,0:T(8,128)(2,1)S(1)}, u32[]{:S(2)}, u32[]{:S(2)}) collective-permute-start(bf16[320,384]{1,0:T(8,128)(2,1)S(1)} %collective-permute-done.15), channel_id=1, source_target_pairs={{8,0},{10,2},{12,4},{14,6},{16,24},{18,26},{20,28},{22,30},{9,1},{... | collective-permute-start | bytes 737288 | tf_op jit(solution)/shard_map/ppermute | solution.py:22
  17.9 0.1 collective-permute-start.14
  18.0 2.2 %pack.1 = (bf16[2,256,384]{2,1,0:T(8,128)(2,1)}, bf16[2,256,384]{2,1,0:T(8,128)(2,1)}, s32[32,128]{1,0:T(8,128)}) custom-call(s32[12,32]{1,0:T(8,128)} %bitcast.11, s32[1,32]{1,0:T(1,128)} %bitcast.12, bf16[256,384]{1,0:T(8,128)(2,1)} %refs_2_.1, bf16[256,384]{1,0:T(8,128)(2,1)} %refs_3_.1, bf16[256,384]{1,0:T(8,128)(2,1)} %refs_4_.1, bf16[256,384]{1,0:T(8,128)(2,1)} %refs_5_.1), custom_call_target="tpu_custom_call" | custom-call | tf_op jit(solution)/shard_map/pack/pallas_call | solution.py:239
  20.2 1.8 %collective-permute-start.6 = (bf16[2,256,384]{2,1,0:T(8,128)(2,1)}, bf16[2,256,384]{2,1,0:T(8,128)(2,1)S(1)}, u32[]{:S(2)}, u32[]{:S(2)}) collective-permute-start(bf16[2,256,384]{2,1,0:T(8,128)(2,1)} %get-tuple-element.13), channel_id=1, source_target_pairs={{0,4},{2,6},{4,0},{6,2},{8,12},{10,14},{12,8},{14,10},{16,20},{18,... | collective-permute-start | bytes 1179656 | tf_op jit(solution)/shard_map/ppermute | solution.py:22
  22.0 0.0 collective-permute-start.5
  22.0 0.0 collective-permute-done.16
  22.0 0.3 collective-permute-start.1
  22.3 2.0 %collective-permute-done.17 = bf16[320,384]{1,0:T(8,128)(2,1)S(1)} collective-permute-done((bf16[320,384]{1,0:T(8,128)(2,1)S(1)}, bf16[320,384]{1,0:T(8,128)(2,1)S(1)}, u32[]{:S(2)}, u32[]{:S(2)}) %collective-permute-start.17) | collective-permute-done | bytes 245792 | tf_op jit(solution)/shard_map/ppermute | solution.py:22
  24.3 2.8 %collective-permute-done.14 = bf16[320,384]{1,0:T(8,128)(2,1)S(1)} collective-permute-done((bf16[320,384]{1,0:T(8,128)(2,1)}, bf16[320,384]{1,0:T(8,128)(2,1)S(1)}, u32[]{:S(2)}, u32[]{:S(2)}) %collective-permute-start.14) | collective-permute-done | bytes 245792 | tf_op jit(solution)/shard_map/ppermute | solution.py:22
  27.1 0.1 broadcast_select_fusion
  27.2 1.3 %collective-permute-start.21 = (bf16[2,320,384]{2,1,0:T(8,128)(2,1)S(1)}, bf16[2,320,384]{2,1,0:T(8,128)(2,1)S(1)}, u32[]{:S(2)}, u32[]{:S(2)}) collective-permute-start(bf16[2,320,384]{2,1,0:T(8,128)(2,1)S(1)} %get-tuple-element.19), channel_id=1, source_target_pairs={{0,1},{1,0},{2,3},{3,2},{4,5},{5,4},{6,7},{7,6},{8,9},{9,8},{10,11... | collective-permute-start | bytes 1474568 | tf_op jit(solution)/shard_map/ppermute | solution.py:26
  28.6 0.0 collective-permute-start
  28.6 3.8 %collective-permute-done.6.b2 = bf16[2,256,384]{2,1,0:T(8,128)(2,1)S(1)} collective-permute-done((bf16[2,256,384]{2,1,0:T(8,128)(2,1)}, bf16[2,256,384]{2,1,0:T(8,128)(2,1)S(1)}, u32[]{:S(2)}, u32[]{:S(2)}) %collective-permute-start.6) | collective-permute-done | bytes 393248 | tf_op jit(solution)/shard_map/ppermute | solution.py:22
  32.4 3.8 %collective-permute-start.8 = (bf16[2,256,384]{2,1,0:T(8,128)(2,1)S(1)}, bf16[2,256,384]{2,1,0:T(8,128)(2,1)S(1)}, u32[]{:S(2)}, u32[]{:S(2)}) collective-permute-start(bf16[2,256,384]{2,1,0:T(8,128)(2,1)S(1)} %collective-permute-done.6.b2), channel_id=1, source_target_pairs={{0,8},{2,10},{8,16},{10,18},{12,4},{14,6},{16,24},{18,26},{20,12},... | collective-permute-start | bytes 1179656 | tf_op jit(solution)/shard_map/ppermute | solution.py:22
  36.2 0.0 collective-permute-done.5.b1
  36.2 0.0 copy-start.11
  36.2 0.1 collective-permute-start.7
  36.3 1.7 %collective-permute-done.1.refs_7_ = bf16[2,256,384]{2,1,0:T(8,128)(2,1)S(1)} collective-permute-done((bf16[2,256,384]{2,1,0:T(8,128)(2,1)}, bf16[2,256,384]{2,1,0:T(8,128)(2,1)S(1)}, u32[]{:S(2)}, u32[]{:S(2)}) %collective-permute-start.1) | collective-permute-done | bytes 393248 | tf_op jit(solution)/shard_map/ppermute | solution.py:22
  38.0 5.3 %collective-permute-start.3 = (bf16[2,256,384]{2,1,0:T(8,128)(2,1)S(1)}, bf16[2,256,384]{2,1,0:T(8,128)(2,1)}, u32[]{:S(2)}, u32[]{:S(2)}) collective-permute-start(bf16[2,256,384]{2,1,0:T(8,128)(2,1)S(1)} %collective-permute-done.1.refs_7_), channel_id=1, source_target_pairs={{0,8},{2,10},{8,16},{10,18},{12,4},{14,6},{16,24},{18,26},{20,12},... | collective-permute-start | bytes 1179656 | tf_op jit(solution)/shard_map/ppermute | solution.py:22
  43.3 0.0 collective-permute-done.refs_6_
  43.3 0.1 collective-permute-start.19
  43.4 0.0 collective-permute-done.21.refs_21_
  43.4 2.0 %collective-permute-start.23 = (bf16[2,320,384]{2,1,0:T(8,128)(2,1)S(1)}, bf16[2,320,384]{2,1,0:T(8,128)(2,1)S(1)}, u32[]{:S(2)}, u32[]{:S(2)}) collective-permute-start(bf16[2,320,384]{2,1,0:T(8,128)(2,1)S(1)} %collective-permute-done.21.refs_21_), channel_id=1, source_target_pairs={{0,4},{2,6},{4,0},{6,2},{8,12},{10,14},{12,8},{14,10},{16,20},{18,... | collective-permute-start | bytes 1474568 | tf_op jit(solution)/shard_map/ppermute | solution.py:22
  45.4 0.0 collective-permute-done.8.b4
  45.4 0.0 collective-permute-start.2
  45.4 0.0 collective-permute-done.7.b3
  45.4 0.5 collective-permute-start.9
  45.9 0.0 copy-done.10
  45.9 5.6 %collective-permute-done.3.refs_9_ = bf16[2,256,384]{2,1,0:T(8,128)(2,1)} collective-permute-done((bf16[2,256,384]{2,1,0:T(8,128)(2,1)S(1)}, bf16[2,256,384]{2,1,0:T(8,128)(2,1)}, u32[]{:S(2)}, u32[]{:S(2)}) %collective-permute-start.3) | collective-permute-done | bytes 393248 | tf_op jit(solution)/shard_map/ppermute | solution.py:22
  51.5 0.0 collective-permute-start.18
  51.5 0.0 collective-permute-done.2.refs_8_
  51.6 0.5 collective-permute-start.22
  52.1 5.4 %collective-permute-done.19.refs_19_ = bf16[2,320,384]{2,1,0:T(8,128)(2,1)S(1)} collective-permute-done((bf16[2,320,384]{2,1,0:T(8,128)(2,1)S(1)}, bf16[2,320,384]{2,1,0:T(8,128)(2,1)S(1)}, u32[]{:S(2)}, u32[]{:S(2)}) %collective-permute-start.19) | collective-permute-done | bytes 491552 | tf_op jit(solution)/shard_map/ppermute | solution.py:22
  57.5 0.0 collective-permute-start.20
  57.5 8.1 %collective-permute-done.23.refs_23_ = bf16[2,320,384]{2,1,0:T(8,128)(2,1)S(1)} collective-permute-done((bf16[2,320,384]{2,1,0:T(8,128)(2,1)S(1)}, bf16[2,320,384]{2,1,0:T(8,128)(2,1)S(1)}, u32[]{:S(2)}, u32[]{:S(2)}) %collective-permute-start.23) | collective-permute-done | bytes 491552 | tf_op jit(solution)/shard_map/ppermute | solution.py:22
  65.5 0.0 copy-done.7
  65.5 0.0 collective-permute-start.24
  65.6 0.0 collective-permute-done.9.b5
  65.6 0.6 collective-permute-start.4
  66.2 0.2 copy-done.14
  66.4 5.8 %query_pass.1 = (bf16[256,384]{1,0:T(8,128)(2,1)}, f32[8,256]{1,0:T(8,128)}) custom-call(s32[1]{0:T(128)} %bitcast.at_ref.refs_0_, s32[32,128]{1,0:T(8,128)} %get-tuple-element.11.lists_ref.refs_1_, bf16[256,384]{1,0:T(8,128)(2,1)} %refs_4_.1, bf16[256,384]{1,0:T(8,128)(2,1)} %refs_5_.1, bf16[256,384]{1,0:T(8,128)(2,1)} %refs_2_.1, ...), custom_call_target="tpu_custom_call" | custom-call | tf_op jit(solution)/shard_map/query_pass/pallas_call | solution.py:192
  72.2 0.0 collective-permute-done.18.refs_18_
  72.2 0.0 copy-start.4
  72.2 0.5 collective-permute-start.10
  72.7 1.0 %collective-permute-done.10.refs_12_ = f32[8,256]{1,0:T(8,128)S(1)} collective-permute-done((f32[8,256]{1,0:T(8,128)}, f32[8,256]{1,0:T(8,128)S(1)}, u32[]{:S(2)}, u32[]{:S(2)}) %collective-permute-start.10) | collective-permute-done | bytes 8224 | tf_op jit(solution)/shard_map/ppermute | solution.py:22
  73.8 1.5 %collective-permute-start.13 = (bf16[256,384]{1,0:T(8,128)(2,1)}, bf16[256,384]{1,0:T(8,128)(2,1)S(1)}, u32[]{:S(2)}, u32[]{:S(2)}) collective-permute-start(bf16[256,384]{1,0:T(8,128)(2,1)} %get-tuple-element.15.refs_15_), channel_id=1, source_target_pairs={{0,1},{1,0},{2,3},{3,2},{4,5},{5,4},{6,7},{7,6},{8,9},{9,8},{10,11... | collective-permute-start | bytes 589832 | tf_op jit(solution)/shard_map/ppermute | solution.py:26
  75.3 0.7 constant_dynamic-update-slice_fusion.1
  76.0 0.0 collective-permute-done.4.refs_10_
  76.0 0.3 collective-permute-start.11
  76.2 3.5 %collective-permute-done.11.refs_13_ = f32[16,256]{1,0:T(8,128)S(1)} collective-permute-done((f32[16,256]{1,0:T(8,128)S(1)}, f32[16,256]{1,0:T(8,128)S(1)}, u32[]{:S(2)}, u32[]{:S(2)}) %collective-permute-start.11) | collective-permute-done | bytes 16416 | tf_op jit(solution)/shard_map/ppermute | solution.py:22
  79.7 1.9 %collective-permute-start.12 = (f32[16,256]{1,0:T(8,128)S(1)}, f32[16,256]{1,0:T(8,128)S(1)}, u32[]{:S(2)}, u32[]{:S(2)}) collective-permute-start(f32[16,256]{1,0:T(8,128)S(1)} %constant_dynamic-update-slice_fusion), channel_id=1, source_target_pairs={{4,8},{6,10},{8,4},{10,6},{12,16},{14,18},{16,12},{18,14},{20,24},... | collective-permute-start | bytes 49160 | tf_op jit(solution)/shard_map/ppermute | solution.py:22
  81.6 4.6 %collective-permute-done.12.refs_14_ = f32[16,256]{1,0:T(8,128)S(1)} collective-permute-done((f32[16,256]{1,0:T(8,128)S(1)}, f32[16,256]{1,0:T(8,128)S(1)}, u32[]{:S(2)}, u32[]{:S(2)}) %collective-permute-start.12) | collective-permute-done | bytes 16416 | tf_op jit(solution)/shard_map/ppermute | solution.py:22
  86.2 0.0 collective-permute-done.13.refs_16_
  86.2 0.0 collective-permute-done.20.refs_20_
  86.2 0.0 collective-permute-done.22.refs_22_
  86.3 0.0 collective-permute-done.24.refs_24_
  86.3 0.5 copy-done.19
  86.8 0.1 copy-done.16
  86.9 0.2 copy-done.6
  87.1 0.2 copy-done.5
  87.3 9.6 %final_pass.1 = (bf16[256,384]{1,0:T(8,128)(2,1)}, bf16[256,384]{1,0:T(8,128)(2,1)}, bf16[256,2560]{1,0:T(8,128)(2,1)}) custom-call(s32[1]{0:T(128)} %bitcast.at_ref.refs_0_, s32[32,128]{1,0:T(8,128)} %get-tuple-element.11.lists_ref.refs_1_, bf16[256,384]{1,0:T(8,128)(2,1)} %refs_2_.1, bf16[256,384]{1,0:T(8,128)(2,1)} %refs_3_.1, bf16[256,384]{1,0:T(8,128)(2,1)} %refs_4_.1, ...), custom_call_target="tpu_custom_call" | custom-call | tf_op jit(solution)/shard_map/final_pass/pallas_call | solution.py:296
  (35 shorter events, 0.1 us)
Async XLA Ops:
  0.6 26.4 %copy-start.15 = (bf16[320,384]{1,0:T(8,128)(2,1)S(1)}, bf16[320,384]{1,0:T(8,128)(2,1)}, u32[]{:S(2)}) copy-start(bf16[320,384]{1,0:T(8,128)(2,1)} %param.11) | copy-start | bytes 737284
  0.6 13.4 %collective-permute-start.15 = (bf16[320,384]{1,0:T(8,128)(2,1)}, bf16[320,384]{1,0:T(8,128)(2,1)S(1)}, u32[]{:S(2)}, u32[]{:S(2)}) collective-permute-start(bf16[320,384]{1,0:T(8,128)(2,1)} %param.11), channel_id=1, source_target_pairs={{0,16},{2,18},{4,20},{6,22},{8,24},{10,26},{12,28},{14,30},{16,0},... | collective-permute-start | bytes 737288 | tf_op jit(solution)/shard_map/ppermute | solution.py:22
  3.3 18.7 %collective-permute-start.16 = (bf16[320,384]{1,0:T(8,128)(2,1)}, bf16[320,384]{1,0:T(8,128)(2,1)S(1)}, u32[]{:S(2)}, u32[]{:S(2)}) collective-permute-start(bf16[320,384]{1,0:T(8,128)(2,1)} %param.11), channel_id=1, source_target_pairs={{8,16},{10,18},{12,20},{14,22},{16,8},{18,10},{20,12},{22,14},{9,1... | collective-permute-start | bytes 737288 | tf_op jit(solution)/shard_map/ppermute | solution.py:22
  14.1 10.2 %collective-permute-start.17 = (bf16[320,384]{1,0:T(8,128)(2,1)S(1)}, bf16[320,384]{1,0:T(8,128)(2,1)S(1)}, u32[]{:S(2)}, u32[]{:S(2)}) collective-permute-start(bf16[320,384]{1,0:T(8,128)(2,1)S(1)} %collective-permute-done.15), channel_id=1, source_target_pairs={{8,0},{10,2},{12,4},{14,6},{16,24},{18,26},{20,28},{22,30},{9,1},{... | collective-permute-start | bytes 737288 | tf_op jit(solution)/shard_map/ppermute | solution.py:22
  17.9 9.1 %collective-permute-start.14 = (bf16[320,384]{1,0:T(8,128)(2,1)}, bf16[320,384]{1,0:T(8,128)(2,1)S(1)}, u32[]{:S(2)}, u32[]{:S(2)}) collective-permute-start(bf16[320,384]{1,0:T(8,128)(2,1)} %param.11), channel_id=1, source_target_pairs={{0,8},{2,10},{4,12},{6,14},{8,0},{10,2},{12,4},{14,6},{16,24},{18,... | collective-permute-start | bytes 737288 | tf_op jit(solution)/shard_map/ppermute | solution.py:22
  20.2 12.2 %collective-permute-start.6 = (bf16[2,256,384]{2,1,0:T(8,128)(2,1)}, bf16[2,256,384]{2,1,0:T(8,128)(2,1)S(1)}, u32[]{:S(2)}, u32[]{:S(2)}) collective-permute-start(bf16[2,256,384]{2,1,0:T(8,128)(2,1)} %get-tuple-element.13), channel_id=1, source_target_pairs={{0,4},{2,6},{4,0},{6,2},{8,12},{10,14},{12,8},{14,10},{16,20},{18,... | collective-permute-start | bytes 1179656 | tf_op jit(solution)/shard_map/ppermute | solution.py:22
  22.0 14.2 %collective-permute-start.5 = (bf16[2,256,384]{2,1,0:T(8,128)(2,1)}, bf16[2,256,384]{2,1,0:T(8,128)(2,1)S(1)}, u32[]{:S(2)}, u32[]{:S(2)}) collective-permute-start(bf16[2,256,384]{2,1,0:T(8,128)(2,1)} %get-tuple-element.13), channel_id=1, source_target_pairs={{0,2},{2,0},{4,6},{6,4},{8,10},{10,8},{12,14},{14,12},{16,18},{18,... | collective-permute-start | bytes 1179656 | tf_op jit(solution)/shard_map/ppermute | solution.py:22
  22.0 6.6 %copy-start.20 = (bf16[2,256,384]{2,1,0:T(8,128)(2,1)S(1)}, bf16[2,256,384]{2,1,0:T(8,128)(2,1)}, u32[]{:S(2)}) copy-start(bf16[2,256,384]{2,1,0:T(8,128)(2,1)} %get-tuple-element.12) | copy-start | bytes 1179652
  22.0 15.9 %collective-permute-start.1 = (bf16[2,256,384]{2,1,0:T(8,128)(2,1)}, bf16[2,256,384]{2,1,0:T(8,128)(2,1)S(1)}, u32[]{:S(2)}, u32[]{:S(2)}) collective-permute-start(bf16[2,256,384]{2,1,0:T(8,128)(2,1)} %get-tuple-element.12), channel_id=1, source_target_pairs={{0,4},{2,6},{4,0},{6,2},{8,12},{10,14},{12,8},{14,10},{16,20},{18,... | collective-permute-start | bytes 1179656 | tf_op jit(solution)/shard_map/ppermute | solution.py:22
  27.2 45.0 %copy-start = (bf16[2,320,384]{2,1,0:T(8,128)(2,1)}, bf16[2,320,384]{2,1,0:T(8,128)(2,1)S(1)}, u32[]{:S(2)}) copy-start(bf16[2,320,384]{2,1,0:T(8,128)(2,1)S(1)} %get-tuple-element.20.refs_17_) | copy-start | bytes 1474564
  27.2 16.2 %collective-permute-start.21 = (bf16[2,320,384]{2,1,0:T(8,128)(2,1)S(1)}, bf16[2,320,384]{2,1,0:T(8,128)(2,1)S(1)}, u32[]{:S(2)}, u32[]{:S(2)}) collective-permute-start(bf16[2,320,384]{2,1,0:T(8,128)(2,1)S(1)} %get-tuple-element.19), channel_id=1, source_target_pairs={{0,1},{1,0},{2,3},{3,2},{4,5},{5,4},{6,7},{7,6},{8,9},{9,8},{10,11... | collective-permute-start | bytes 1474568 | tf_op jit(solution)/shard_map/ppermute | solution.py:26
  28.6 14.7 %collective-permute-start = (bf16[2,256,384]{2,1,0:T(8,128)(2,1)S(1)}, bf16[2,256,384]{2,1,0:T(8,128)(2,1)S(1)}, u32[]{:S(2)}, u32[]{:S(2)}) collective-permute-start(bf16[2,256,384]{2,1,0:T(8,128)(2,1)S(1)} %copy-done.20), channel_id=1, source_target_pairs={{0,2},{2,0},{4,6},{6,4},{8,10},{10,8},{12,14},{14,12},{16,18},{18,... | collective-permute-start | bytes 1179656 | tf_op jit(solution)/shard_map/ppermute | solution.py:22
  32.4 13.5 %copy-start.10 = (bf16[2,256,384]{2,1,0:T(8,128)(2,1)}, bf16[2,256,384]{2,1,0:T(8,128)(2,1)S(1)}, u32[]{:S(2)}) copy-start(bf16[2,256,384]{2,1,0:T(8,128)(2,1)S(1)} %collective-permute-done.6.b2) | copy-start | bytes 1179652
  32.4 13.0 %collective-permute-start.8 = (bf16[2,256,384]{2,1,0:T(8,128)(2,1)S(1)}, bf16[2,256,384]{2,1,0:T(8,128)(2,1)S(1)}, u32[]{:S(2)}, u32[]{:S(2)}) collective-permute-start(bf16[2,256,384]{2,1,0:T(8,128)(2,1)S(1)} %collective-permute-done.6.b2), channel_id=1, source_target_pairs={{0,8},{2,10},{8,16},{10,18},{12,4},{14,6},{16,24},{18,26},{20,12},... | collective-permute-start | bytes 1179656 | tf_op jit(solution)/shard_map/ppermute | solution.py:22
  36.2 7.1 %copy-start.11 = (bf16[2,256,384]{2,1,0:T(8,128)(2,1)}, bf16[2,256,384]{2,1,0:T(8,128)(2,1)S(1)}, u32[]{:S(2)}) copy-start(bf16[2,256,384]{2,1,0:T(8,128)(2,1)S(1)} %collective-permute-done.5.b1) | copy-start | bytes 1179652
  36.2 9.2 %collective-permute-start.7 = (bf16[2,256,384]{2,1,0:T(8,128)(2,1)S(1)}, bf16[2,256,384]{2,1,0:T(8,128)(2,1)S(1)}, u32[]{:S(2)}, u32[]{:S(2)}) collective-permute-start(bf16[2,256,384]{2,1,0:T(8,128)(2,1)S(1)} %collective-permute-done.6.b2), channel_id=1, source_target_pairs={{0,2},{2,0},{4,6},{6,4},{8,10},{10,8},{12,14},{14,12},{16,18},{18,... | collective-permute-start | bytes 1179656 | tf_op jit(solution)/shard_map/ppermute | solution.py:22
  38.0 27.6 %copy-start.7 = (bf16[2,256,384]{2,1,0:T(8,128)(2,1)}, bf16[2,256,384]{2,1,0:T(8,128)(2,1)S(1)}, u32[]{:S(2)}) copy-start(bf16[2,256,384]{2,1,0:T(8,128)(2,1)S(1)} %collective-permute-done.1.refs_7_) | copy-start | bytes 1179652
  38.0 13.6 %collective-permute-start.3 = (bf16[2,256,384]{2,1,0:T(8,128)(2,1)S(1)}, bf16[2,256,384]{2,1,0:T(8,128)(2,1)}, u32[]{:S(2)}, u32[]{:S(2)}) collective-permute-start(bf16[2,256,384]{2,1,0:T(8,128)(2,1)S(1)} %collective-permute-done.1.refs_7_), channel_id=1, source_target_pairs={{0,8},{2,10},{8,16},{10,18},{12,4},{14,6},{16,24},{18,26},{20,12},... | collective-permute-start | bytes 1179656 | tf_op jit(solution)/shard_map/ppermute | solution.py:22
  43.3 22.3 %copy-start.8 = (bf16[2,256,384]{2,1,0:T(8,128)(2,1)}, bf16[2,256,384]{2,1,0:T(8,128)(2,1)S(1)}, u32[]{:S(2)}) copy-start(bf16[2,256,384]{2,1,0:T(8,128)(2,1)S(1)} %collective-permute-done.refs_6_) | copy-start | bytes 1179652
  43.3 14.2 %collective-permute-start.19 = (bf16[2,320,384]{2,1,0:T(8,128)(2,1)S(1)}, bf16[2,320,384]{2,1,0:T(8,128)(2,1)S(1)}, u32[]{:S(2)}, u32[]{:S(2)}) collective-permute-start(bf16[2,320,384]{2,1,0:T(8,128)(2,1)S(1)} %get-tuple-element.20.refs_17_), channel_id=1, source_target_pairs={{0,4},{2,6},{4,0},{6,2},{8,12},{10,14},{12,8},{14,10},{16,20},{18,... | collective-permute-start | bytes 1474568 | tf_op jit(solution)/shard_map/ppermute | solution.py:22
  43.4 28.8 %copy-start.1 = (bf16[2,320,384]{2,1,0:T(8,128)(2,1)}, bf16[2,320,384]{2,1,0:T(8,128)(2,1)S(1)}, u32[]{:S(2)}) copy-start(bf16[2,320,384]{2,1,0:T(8,128)(2,1)S(1)} %collective-permute-done.21.refs_21_) | copy-start | bytes 1474564
  43.4 22.1 %collective-permute-start.23 = (bf16[2,320,384]{2,1,0:T(8,128)(2,1)S(1)}, bf16[2,320,384]{2,1,0:T(8,128)(2,1)S(1)}, u32[]{:S(2)}, u32[]{:S(2)}) collective-permute-start(bf16[2,320,384]{2,1,0:T(8,128)(2,1)S(1)} %collective-permute-done.21.refs_21_), channel_id=1, source_target_pairs={{0,4},{2,6},{4,0},{6,2},{8,12},{10,14},{12,8},{14,10},{16,20},{18,... | collective-permute-start | bytes 1474568 | tf_op jit(solution)/shard_map/ppermute | solution.py:22
  45.4 20.7 %copy-start.12 = (bf16[2,256,384]{2,1,0:T(8,128)(2,1)}, bf16[2,256,384]{2,1,0:T(8,128)(2,1)S(1)}, u32[]{:S(2)}) copy-start(bf16[2,256,384]{2,1,0:T(8,128)(2,1)S(1)} %collective-permute-done.8.b4) | copy-start | bytes 1179652
  45.4 6.1 %collective-permute-start.2 = (bf16[2,256,384]{2,1,0:T(8,128)(2,1)S(1)}, bf16[2,256,384]{2,1,0:T(8,128)(2,1)S(1)}, u32[]{:S(2)}, u32[]{:S(2)}) collective-permute-start(bf16[2,256,384]{2,1,0:T(8,128)(2,1)S(1)} %collective-permute-done.1.refs_7_), channel_id=1, source_target_pairs={{0,2},{2,0},{4,6},{6,4},{8,10},{10,8},{12,14},{14,12},{16,18},{18,... | collective-permute-start | bytes 1179656 | tf_op jit(solution)/shard_map/ppermute | solution.py:22
  45.4 20.7 %copy-start.13 = (bf16[2,256,384]{2,1,0:T(8,128)(2,1)}, bf16[2,256,384]{2,1,0:T(8,128)(2,1)S(1)}, u32[]{:S(2)}) copy-start(bf16[2,256,384]{2,1,0:T(8,128)(2,1)S(1)} %collective-permute-done.7.b3) | copy-start | bytes 1179652
  45.4 20.1 %collective-permute-start.9 = (bf16[2,256,384]{2,1,0:T(8,128)(2,1)S(1)}, bf16[2,256,384]{2,1,0:T(8,128)(2,1)S(1)}, u32[]{:S(2)}, u32[]{:S(2)}) collective-permute-start(bf16[2,256,384]{2,1,0:T(8,128)(2,1)S(1)} %collective-permute-done.8.b4), channel_id=1, source_target_pairs={{0,2},{2,0},{4,6},{6,4},{8,10},{10,8},{12,14},{14,12},{16,18},{18,... | collective-permute-start | bytes 1179656 | tf_op jit(solution)/shard_map/ppermute | solution.py:22
  51.5 20.7 %collective-permute-start.18 = (bf16[2,320,384]{2,1,0:T(8,128)(2,1)S(1)}, bf16[2,320,384]{2,1,0:T(8,128)(2,1)S(1)}, u32[]{:S(2)}, u32[]{:S(2)}) collective-permute-start(bf16[2,320,384]{2,1,0:T(8,128)(2,1)S(1)} %get-tuple-element.20.refs_17_), channel_id=1, source_target_pairs={{0,2},{2,0},{4,6},{6,4},{8,10},{10,8},{12,14},{14,12},{16,18},{18,... | collective-permute-start | bytes 1474568 | tf_op jit(solution)/shard_map/ppermute | solution.py:22
  51.6 14.0 %copy-start.9 = (bf16[2,256,384]{2,1,0:T(8,128)(2,1)}, bf16[2,256,384]{2,1,0:T(8,128)(2,1)S(1)}, u32[]{:S(2)}) copy-start(bf16[2,256,384]{2,1,0:T(8,128)(2,1)S(1)} %collective-permute-done.2.refs_8_) | copy-start | bytes 1179652
  51.6 34.7 %collective-permute-start.22 = (bf16[2,320,384]{2,1,0:T(8,128)(2,1)S(1)}, bf16[2,320,384]{2,1,0:T(8,128)(2,1)S(1)}, u32[]{:S(2)}, u32[]{:S(2)}) collective-permute-start(bf16[2,320,384]{2,1,0:T(8,128)(2,1)S(1)} %collective-permute-done.21.refs_21_), channel_id=1, source_target_pairs={{0,2},{2,0},{4,6},{6,4},{8,10},{10,8},{12,14},{14,12},{16,18},{18,... | collective-permute-start | bytes 1474568 | tf_op jit(solution)/shard_map/ppermute | solution.py:22
  57.5 14.7 %copy-start.2 = (bf16[2,320,384]{2,1,0:T(8,128)(2,1)}, bf16[2,320,384]{2,1,0:T(8,128)(2,1)S(1)}, u32[]{:S(2)}) copy-start(bf16[2,320,384]{2,1,0:T(8,128)(2,1)S(1)} %collective-permute-done.19.refs_19_) | copy-start | bytes 1474564
  57.5 28.8 %collective-permute-start.20 = (bf16[2,320,384]{2,1,0:T(8,128)(2,1)S(1)}, bf16[2,320,384]{2,1,0:T(8,128)(2,1)S(1)}, u32[]{:S(2)}, u32[]{:S(2)}) collective-permute-start(bf16[2,320,384]{2,1,0:T(8,128)(2,1)S(1)} %collective-permute-done.19.refs_19_), channel_id=1, source_target_pairs={{0,2},{2,0},{4,6},{6,4},{8,10},{10,8},{12,14},{14,12},{16,18},{18,... | collective-permute-start | bytes 1474568 | tf_op jit(solution)/shard_map/ppermute | solution.py:22
  65.5 6.6 %copy-start.3 = (bf16[2,320,384]{2,1,0:T(8,128)(2,1)}, bf16[2,320,384]{2,1,0:T(8,128)(2,1)S(1)}, u32[]{:S(2)}) copy-start(bf16[2,320,384]{2,1,0:T(8,128)(2,1)S(1)} %collective-permute-done.23.refs_23_) | copy-start | bytes 1474564
  65.5 20.7 %collective-permute-start.24 = (bf16[2,320,384]{2,1,0:T(8,128)(2,1)S(1)}, bf16[2,320,384]{2,1,0:T(8,128)(2,1)}, u32[]{:S(2)}, u32[]{:S(2)}) collective-permute-start(bf16[2,320,384]{2,1,0:T(8,128)(2,1)S(1)} %collective-permute-done.23.refs_23_), channel_id=1, source_target_pairs={{0,2},{2,0},{4,6},{6,4},{8,10},{10,8},{12,14},{14,12},{16,18},{18,... | collective-permute-start | bytes 1474568 | tf_op jit(solution)/shard_map/ppermute | solution.py:22
  65.6 0.8 copy-start.14
  65.6 10.4 %collective-permute-start.4 = (bf16[2,256,384]{2,1,0:T(8,128)(2,1)}, bf16[2,256,384]{2,1,0:T(8,128)(2,1)}, u32[]{:S(2)}, u32[]{:S(2)}) collective-permute-start(bf16[2,256,384]{2,1,0:T(8,128)(2,1)} %collective-permute-done.3.refs_9_), channel_id=1, source_target_pairs={{0,2},{2,0},{4,6},{6,4},{8,10},{10,8},{12,14},{14,12},{16,18},{18,... | collective-permute-start | bytes 1179656 | tf_op jit(solution)/shard_map/ppermute | solution.py:22
  72.2 14.1 %copy-start.4 = (bf16[2,320,384]{2,1,0:T(8,128)(2,1)}, bf16[2,320,384]{2,1,0:T(8,128)(2,1)S(1)}, u32[]{:S(2)}) copy-start(bf16[2,320,384]{2,1,0:T(8,128)(2,1)S(1)} %collective-permute-done.18.refs_18_) | copy-start | bytes 1474564
  72.2 1.5 %collective-permute-start.10 = (f32[8,256]{1,0:T(8,128)}, f32[8,256]{1,0:T(8,128)S(1)}, u32[]{:S(2)}, u32[]{:S(2)}) collective-permute-start(f32[8,256]{1,0:T(8,128)} %get-tuple-element.14.refs_11_), channel_id=1, source_target_pairs={{0,2},{2,0},{4,6},{6,4},{8,10},{10,8},{12,14},{14,12},{16,18},{18,... | collective-permute-start | bytes 24584 | tf_op jit(solution)/shard_map/ppermute | solution.py:22
  73.8 12.5 %copy-start.17 = (f32[8,256]{1,0:T(8,128)}, f32[8,256]{1,0:T(8,128)S(1)}, u32[]{:S(2)}) copy-start(f32[8,256]{1,0:T(8,128)S(1)} %collective-permute-done.10.refs_12_) | copy-start | bytes 24580
  73.8 12.5 %collective-permute-start.13 = (bf16[256,384]{1,0:T(8,128)(2,1)}, bf16[256,384]{1,0:T(8,128)(2,1)S(1)}, u32[]{:S(2)}, u32[]{:S(2)}) collective-permute-start(bf16[256,384]{1,0:T(8,128)(2,1)} %get-tuple-element.15.refs_15_), channel_id=1, source_target_pairs={{0,1},{1,0},{2,3},{3,2},{4,5},{5,4},{6,7},{7,6},{8,9},{9,8},{10,11... | collective-permute-start | bytes 589832 | tf_op jit(solution)/shard_map/ppermute | solution.py:26
  76.0 3.7 %collective-permute-start.11 = (f32[16,256]{1,0:T(8,128)S(1)}, f32[16,256]{1,0:T(8,128)S(1)}, u32[]{:S(2)}, u32[]{:S(2)}) collective-permute-start(f32[16,256]{1,0:T(8,128)S(1)} %constant_dynamic-update-slice_fusion), channel_id=1, source_target_pairs={{0,4},{2,6},{4,0},{6,2},{8,12},{10,14},{12,8},{14,10},{16,20},{18,... | collective-permute-start | bytes 49160 | tf_op jit(solution)/shard_map/ppermute | solution.py:22
  79.7 6.6 %copy-start.18 = (f32[16,256]{1,0:T(8,128)}, f32[16,256]{1,0:T(8,128)S(1)}, u32[]{:S(2)}) copy-start(f32[16,256]{1,0:T(8,128)S(1)} %collective-permute-done.11.refs_13_) | copy-start | bytes 49156
  79.7 6.5 %collective-permute-start.12 = (f32[16,256]{1,0:T(8,128)S(1)}, f32[16,256]{1,0:T(8,128)S(1)}, u32[]{:S(2)}, u32[]{:S(2)}) collective-permute-start(f32[16,256]{1,0:T(8,128)S(1)} %constant_dynamic-update-slice_fusion), channel_id=1, source_target_pairs={{4,8},{6,10},{8,4},{10,6},{12,16},{14,18},{16,12},{18,14},{20,24},... | collective-permute-start | bytes 49160 | tf_op jit(solution)/shard_map/ppermute | solution.py:22
  86.2 0.6 copy-start.19
  86.2 0.7 copy-start.16
  86.2 0.8 copy-start.6
  86.3 1.0 %copy-start.5 = (bf16[2,320,384]{2,1,0:T(8,128)(2,1)}, bf16[2,320,384]{2,1,0:T(8,128)(2,1)S(1)}, u32[]{:S(2)}) copy-start(bf16[2,320,384]{2,1,0:T(8,128)(2,1)S(1)} %collective-permute-done.22.refs_22_) | copy-start | bytes 1474564

commit v2 on v1

--- a/solution.py
+++ b/solution.py
@@ -88,49 +88,64 @@
     stat_ref[...] = jnp.zeros_like(stat_ref)
     half = q_ref.shape[0] // TILES_DEV
     pairs = [b1, b2, b3, b4, b5]
-    tiles = [(b, a) for b in range(BLOCKS) for a in range(TILES_DEV)]
 
     def mask(b, a):
         at = TILES_DEV * b + a
         return jnp.concatenate([mask_ref[0, at : at + 1], mask_ref[1, at : at + 1]], axis=1)
 
-    for head in range(HEADS_DEV):
-        cols = slice(head * HEAD_DIM, (head + 1) * HEAD_DIM)
-        query = q_ref[:, cols]
-        grad = g_ref[:, cols]
-
-        def key(b):
-            return k_ref[:, cols] if b == 0 else pairs[b - 1][0, :, cols]
-
-        def value(b):
-            return v_ref[:, cols] if b == 0 else pairs[b - 1][1, :, cols]
-
-        top = None
+    def columns(head):
+        return slice(head * HEAD_DIM, (head + 1) * HEAD_DIM)
+
+    def key(head, b):
+        return k_ref[:, columns(head)] if b == 0 else pairs[b - 1][0, :, columns(head)]
+
+    def value(head, b):
+        return v_ref[:, columns(head)] if b == 0 else pairs[b - 1][1, :, columns(head)]
+
+    top = [None] * HEADS_DEV
+    total = [0.0] * HEADS_DEV
+    delta = [0.0] * HEADS_DEV
+    acc = [0.0] * HEADS_DEV
+
+    def products(head, b):
+        scores = nt(key(head, b), q_ref[:, columns(head)])
+        s_ref[head, b] = scores
+        d_ref[head, b] = nt(value(head, b), g_ref[:, columns(head)])
+        for a in range(TILES_DEV):
+            peak = jnp.max(scores[a * half : (a + 1) * half], axis=0, keepdims=True)
+            peak = peak * SCALE_2 + mask(b, a)
+            top[head] = peak if top[head] is None else jnp.maximum(top[head], peak)
+
+    def weigh(head, b):
+        for a in range(TILES_DEV):
+            part = slice(a * half, (a + 1) * half)
+            weight = jnp.exp2(s_ref[head, b, part] * SCALE_2 - (top[head] - mask(b, a)))
+            s_ref[head, b, part] = weight
+            dprobs = d_ref[head, b, part]
+            total[head] = total[head] + jnp.sum(weight, axis=0, keepdims=True)
+            delta[head] = delta[head] + jnp.sum(weight * dprobs, axis=0, keepdims=True)
+
+    def gather(head, b):
+        dscores = (s_ref[head, b] * (d_ref[head, b] - delta[head])).astype(jnp.bfloat16)
+        acc[head] = acc[head] + tn(key(head, b), dscores)
+
+    for step in range(HEADS_DEV + 2):
         for b in range(BLOCKS):
-            scores = nt(key(b), query)
-            s_ref[b] = scores
-            d_ref[b] = nt(value(b), grad)
-            for a in range(TILES_DEV):
-                peak = jnp.max(scores[a * half : (a + 1) * half], axis=0, keepdims=True)
-                peak = peak * SCALE_2 + mask(b, a)
-                top = peak if top is None else jnp.maximum(top, peak)
-        total = jnp.zeros_like(top)
-        delta = jnp.zeros_like(top)
-        for b, a in tiles:
-            part = slice(a * half, (a + 1) * half)
-            weight = jnp.exp2(s_ref[b, part] * SCALE_2 - (top - mask(b, a)))
-            s_ref[b, part] = weight
-            total = total + jnp.sum(weight, axis=0, keepdims=True)
-            delta = delta + jnp.sum(weight * d_ref[b, part], axis=0, keepdims=True)
-        inverse = 1.0 / total
-        delta = delta * inverse
-        acc = jnp.zeros((HEAD_DIM, query.shape[0]), jnp.float32)
-        for b in range(BLOCKS):
-            dscores = (s_ref[b] * (d_ref[b] - delta)).astype(jnp.bfloat16)
-            acc = acc + tn(key(b), dscores)
-        dq_ref[:, cols] = (acc * (inverse * SCALE)).T.astype(jnp.bfloat16)
-        stat_ref[head : head + 1] = top + jnp.log(total) * LOG2_E
-        stat_ref[head + HEADS_DEV : head + HEADS_DEV + 1] = delta
+            if step < HEADS_DEV:
+                products(step, b)
+            if 0 <= step - 1 < HEADS_DEV:
+                weigh(step - 1, b)
+            if 0 <= step - 2:
+                gather(step - 2, b)
+        if 0 <= step - 1 < HEADS_DEV:
+            head = step - 1
+            delta[head] = delta[head] / total[head]
+            stat_ref[head : head + 1] = top[head] + jnp.log(total[head]) * LOG2_E
+            stat_ref[head + HEADS_DEV : head + HEADS_DEV + 1] = delta[head]
+        if 0 <= step - 2:
+            head = step - 2
+            scaled = acc[head] * (SCALE / total[head])
+            dq_ref[:, columns(head)] = scaled.T.astype(jnp.bfloat16)
 
 
 def key_kernel(
@@ -153,33 +168,52 @@
             + there
             for a in range(TILES_DEV)
         ])
-    for head in range(HEADS_DEV):
+
+    def operands(head, b):
         cols = slice(head * HEAD_DIM, (head + 1) * HEAD_DIM)
-        key = k_ref[:, cols]
-        value = v_ref[:, cols]
-        key_acc = jnp.zeros(key.shape, jnp.float32)
-        value_acc = jnp.zeros(key.shape, jnp.float32)
-        for b in range(BLOCKS):
-            query = q_ref[:, cols] if b == 0 else pairs[b - 1][0, :, cols]
-            grad = g_ref[:, cols] if b == 0 else pairs[b - 1][1, :, cols]
-            stat, at = stats[b]
-            log_norm = stat[at + head : at + head + 1]
-            at += HEADS_DEV
-            delta = stat[at + head : at + head + 1]
-            scores = nt(key, query)
-            dprobs = nt(value, grad)
-            low, dscores = [], []
-            for a in range(TILES_DEV):
-                part = slice(a * half, (a + 1) * half)
-                probs = jnp.exp2(scores[part] * SCALE_2 - (log_norm - masks[b][a]))
-                low.append(probs.astype(jnp.bfloat16))
-                dscores.append((probs * (dprobs[part] - delta)).astype(jnp.bfloat16))
-            low = jnp.concatenate(low, axis=0)
-            dscores = jnp.concatenate(dscores, axis=0)
-            value_acc = value_acc + jnp.dot(low, grad, preferred_element_type=jnp.float32)
-            key_acc = key_acc + jnp.dot(dscores, query, preferred_element_type=jnp.float32)
-        dk_ref[:, cols] = (key_acc * SCALE).astype(jnp.bfloat16)
-        dv_ref[:, cols] = value_acc.astype(jnp.bfloat16)
+        if b == 0:
+            return q_ref[:, cols], g_ref[:, cols]
+        return pairs[b - 1][0, :, cols], pairs[b - 1][1, :, cols]
+
+    def products(head, b):
+        cols = slice(head * HEAD_DIM, (head + 1) * HEAD_DIM)
+        query, grad = operands(head, b)
+        return nt(k_ref[:, cols], query), nt(v_ref[:, cols], grad)
+
+    def soften(head, b, scores, dprobs):
+        stat, at = stats[b]
+        log_norm = stat[at + head : at + head + 1]
+        at += HEADS_DEV
+        delta = stat[at + head : at + head + 1]
+        low, dscores = [], []
+        for a in range(TILES_DEV):
+            part = slice(a * half, (a + 1) * half)
+            probs = jnp.exp2(scores[part] * SCALE_2 - (log_norm - masks[b][a]))
+            low.append(probs.astype(jnp.bfloat16))
+            dscores.append((probs * (dprobs[part] - delta)).astype(jnp.bfloat16))
+        return jnp.concatenate(low, axis=0), jnp.concatenate(dscores, axis=0)
+
+    work = [(head, b) for head in range(HEADS_DEV) for b in range(BLOCKS)]
+    ahead = {}
+    soft = {}
+    for i in range(len(work) + 2):
+        if i < len(work):
+            ahead[i] = products(*work[i])
+        if 1 <= i <= len(work):
+            soft[i - 1] = soften(*work[i - 1], *ahead.pop(i - 1))
+        if i < 2:
+            continue
+        head, b = work[i - 2]
+        low, dscores = soft.pop(i - 2)
+        query, grad = operands(head, b)
+        value_term = jnp.dot(low, grad, preferred_element_type=jnp.float32)
+        key_term = jnp.dot(dscores, query, preferred_element_type=jnp.float32)
+        value_acc = value_term if b == 0 else value_acc + value_term
+        key_acc = key_term if b == 0 else key_acc + key_term
+        if b == BLOCKS - 1:
+            cols = slice(head * HEAD_DIM, (head + 1) * HEAD_DIM)
+            dk_ref[:, cols] = (key_acc * SCALE).astype(jnp.bfloat16)
+            dv_ref[:, cols] = value_acc.astype(jnp.bfloat16)
 
 
 SMEM = pl.BlockSpec(memory_space=pltpu.SMEM)
@@ -197,8 +231,9 @@
             jax.ShapeDtypeStruct((rows, width), jnp.bfloat16),
             jax.ShapeDtypeStruct((8, rows), jnp.float32),
         ],
-        scratch_shapes=[pltpu.VMEM((BLOCKS, rows, rows), jnp.float32)] * 2
+        scratch_shapes=[pltpu.VMEM((HEADS_DEV, BLOCKS, rows, rows), jnp.float32)] * 2
         + [pltpu.VMEM((TILES_DEV, 16, TILE), jnp.float32)],
+        compiler_params=pltpu.CompilerParams(vmem_limit_bytes=24 * 2**20),
         name="query_pass",
     )(at, lists, queries, out_grad, keys, values, *pairs)
 
@@ -245,30 +280,20 @@
     )(slots, counts, keys, values, queries, out_grad)
 
 
-def start_input(at_ref, pieces, w_ref, sems):
+def place_pieces(at_ref, pieces, w_ref):
     rows = pieces[0].shape[1]
-    copies = []
     for j in range(2):
         for i, piece in enumerate(pieces):
             place = (at_ref[0] % 4) ^ (i % 4)
-            copy = pltpu.make_async_copy(
-                piece.at[j],
-                w_ref.at[j, i // 4, pl.ds(pl.multiple_of(place * rows, 64), rows)],
-                sems.at[8 * j + i],
-            )
-            copy.start()
-            copies.append(copy)
-    return copies
-
-
-def finish_input(at_ref, q_ref, x_ref, copies, w_ref, o_ref, out_ref, sems):
+            w_ref[j, i // 4, pl.ds(pl.multiple_of(place * rows, 64), rows)] = piece[j]
+
+
+def input_product(at_ref, q_ref, x_ref, w_ref, o_ref, out_ref, sems):
     span = w_ref.shape[2]
     own = q_ref[...]
     other = x_ref[...]
     outs = []
     for j in range(2):
-        for copy in copies[8 * j : 8 * j + 8]:
-            copy.wait()
         part = nt(own, w_ref[j, 0]) + nt(other, w_ref[j, 1])
         o_ref[j] = part.astype(o_ref.dtype)
         first = pl.multiple_of((at_ref[0] % 8 // 4 ^ j) * span, span)
@@ -284,10 +309,10 @@
     key_args, refs = refs[:15], refs[15:]
     own_ref, other_ref = refs[:2]
     pieces, refs = refs[2:10], refs[10:]
-    dk_ref, dv_ref, out_ref, mask_ref, w_ref, o_ref, sems, out_sems = refs
-    copies = start_input(at_ref, pieces, w_ref, sems)
+    dk_ref, dv_ref, out_ref, mask_ref, w_ref, o_ref, sems = refs
+    place_pieces(at_ref, pieces, w_ref)
     key_kernel(*key_args, dk_ref, dv_ref, mask_ref)
-    finish_input(at_ref, own_ref, other_ref, copies, w_ref, o_ref, out_ref, out_sems)
+    input_product(at_ref, own_ref, other_ref, w_ref, o_ref, out_ref, sems)
 
 
 def final_pass(at, lists, keys, values, queries, out_grad, pairs, stats, own, other, pieces):
@@ -295,7 +320,7 @@
     span = pieces[0].shape[1] * 4
     return pl.pallas_call(
         final_kernel,
-        in_specs=[SMEM] + [VMEM] * 16 + [ANYWHERE] * 8,
+        in_specs=[SMEM] + [VMEM] * 24,
         out_specs=[VMEM, VMEM, ANYWHERE],
         out_shape=[jax.ShapeDtypeStruct((rows, width), jnp.bfloat16)] * 2
         + [jax.ShapeDtypeStruct((rows, 2 * span), jnp.bfloat16)],
@@ -303,9 +328,9 @@
             pltpu.VMEM((TILES_DEV, lists.shape[0], TILE), jnp.float32),
             pltpu.VMEM((2, 2, span, width), jnp.bfloat16),
             pltpu.VMEM((2, rows, span), jnp.bfloat16),
-            pltpu.SemaphoreType.DMA((16,)),
             pltpu.SemaphoreType.DMA((2,)),
         ],
+        compiler_params=pltpu.CompilerParams(vmem_limit_bytes=24 * 2**20),
         name="final_pass",
     )(at, lists, keys, values, queries, out_grad, *pairs, *stats, own, other, *pieces)
 

time: 97.2 us -> 88.9 us (0.915)
  Pallas kernels: 17.5 us -> 11.7 us
  local copies, waits for them, and re-layouts: 1.96 us -> 0.04 us
    pallas_call x1, Pallas kernels: 9.59 us -> 6.12 us  [final_pass(): pl.pallas_call(final_kernel, in_specs=[SMEM] + [VMEM] * 24, out_specs=[VM...]
    pallas_call x1, Pallas kernels: 5.78 us -> 3.43 us  [query_pass(): pl.pallas_call(query_kernel, in_specs=[SMEM] + [VMEM] * 10, out_specs=[VM...]
    unnamed x43 -> x15, local copies, waits for them, and re-layouts: 1.96 us -> 0.04 us
  transfers between devices with their start and end apart: 25 -> 25, of which waited for: 11 -> 11; matrix products, arithmetic and copies ran while one was open for 1% -> 0% of each run, Pallas kernels for 8% -> 6%
where the time goes in v2:
time: 88.9 us; the launch traced here: 88.7 us
  waiting for transfers between devices  47.4 us (53%)
  starting transfers between devices  28.5 us (32%)
  Pallas kernels  11.7 us (13%)
    ppermute x23, waiting for transfers between devices, move(): lax.ppermute(block, 'seq', [(i, j) for i, j in pairs if 0 <= j < size])  47.4 us
    ppermute x23, starting transfers between devices, move(): lax.ppermute(block, 'seq', [(i, j) for i, j in pairs if 0 <= j < size])  25.6 us
    pallas_call x1, Pallas kernels, final_pass(): pl.pallas_call(final_kernel, in_specs=[SMEM] + [VMEM] * 24, out_specs=[VM...  6.12 us
    pallas_call x1, Pallas kernels, query_pass(): pl.pallas_call(query_kernel, in_specs=[SMEM] + [VMEM] * 10, out_specs=[VM...  3.43 us
    ppermute x2, starting transfers between devices, swap_groups(): return lax.ppermute(block, 'head', [(0, 1), (1, 0)])  2.85 us
    pallas_call x1, Pallas kernels, pack(): pl.pallas_call(pack_kernel, in_specs=[VMEM] * 6, out_specs=[VMEM] * 3, ou...  2.17 us
  transfers between devices with their start and end apart: 25, of which 11 were waited for; matrix products, arithmetic and copies ran while one was open for 0% of the time, Pallas kernels for 6%

profile of v2, /device:TPU:8, one launch (start us, length us, event | category | flops | bytes accessed | tf_op | source)
XLA Modules:
  0.0 88.7 jit_solution(12308518411422449283)
XLA Ops:
  0.6 0.0 copy-start.5
  0.6 2.7 %collective-permute-start.15 = (bf16[320,384]{1,0:T(8,128)(2,1)}, bf16[320,384]{1,0:T(8,128)(2,1)S(1)}, u32[]{:S(2)}, u32[]{:S(2)}) collective-permute-start(bf16[320,384]{1,0:T(8,128)(2,1)} %param.11), channel_id=1, source_target_pairs={{0,16},{2,18},{4,20},{6,22},{8,24},{10,26},{12,28},{14,30},{16,0},... | collective-permute-start | bytes 737288 | tf_op jit(solution)/shard_map/ppermute | solution.py:22
  3.3 1.9 %collective-permute-start.16 = (bf16[320,384]{1,0:T(8,128)(2,1)}, bf16[320,384]{1,0:T(8,128)(2,1)S(1)}, u32[]{:S(2)}, u32[]{:S(2)}) collective-permute-start(bf16[320,384]{1,0:T(8,128)(2,1)} %param.11), channel_id=1, source_target_pairs={{8,16},{10,18},{12,20},{14,22},{16,8},{18,10},{20,12},{22,14},{9,1... | collective-permute-start | bytes 737288 | tf_op jit(solution)/shard_map/ppermute | solution.py:22
  5.2 8.9 %collective-permute-done.15 = bf16[320,384]{1,0:T(8,128)(2,1)S(1)} collective-permute-done((bf16[320,384]{1,0:T(8,128)(2,1)}, bf16[320,384]{1,0:T(8,128)(2,1)S(1)}, u32[]{:S(2)}, u32[]{:S(2)}) %collective-permute-start.15) | collective-permute-done | bytes 245792 | tf_op jit(solution)/shard_map/ppermute | solution.py:22
  14.1 3.9 %collective-permute-start.17 = (bf16[320,384]{1,0:T(8,128)(2,1)S(1)}, bf16[320,384]{1,0:T(8,128)(2,1)S(1)}, u32[]{:S(2)}, u32[]{:S(2)}) collective-permute-start(bf16[320,384]{1,0:T(8,128)(2,1)S(1)} %collective-permute-done.15), channel_id=1, source_target_pairs={{8,0},{10,2},{12,4},{14,6},{16,24},{18,26},{20,28},{22,30},{9,1},{... | collective-permute-start | bytes 737288 | tf_op jit(solution)/shard_map/ppermute | solution.py:22
  17.9 0.1 collective-permute-start.14
  18.0 2.2 %pack.1 = (bf16[2,256,384]{2,1,0:T(8,128)(2,1)}, bf16[2,256,384]{2,1,0:T(8,128)(2,1)}, s32[32,128]{1,0:T(8,128)}) custom-call(s32[12,32]{1,0:T(8,128)} %bitcast.11, s32[1,32]{1,0:T(1,128)} %bitcast.12, bf16[256,384]{1,0:T(8,128)(2,1)} %refs_2_.1, bf16[256,384]{1,0:T(8,128)(2,1)} %refs_3_.1, bf16[256,384]{1,0:T(8,128)(2,1)} %refs_4_.1, bf16[256,384]{1,0:T(8,128)(2,1)} %refs_5_.1), custom_call_target="tpu_custom_call" | custom-call | tf_op jit(solution)/shard_map/pack/pallas_call | solution.py:274
  20.2 1.8 %collective-permute-start.6 = (bf16[2,256,384]{2,1,0:T(8,128)(2,1)}, bf16[2,256,384]{2,1,0:T(8,128)(2,1)S(1)}, u32[]{:S(2)}, u32[]{:S(2)}) collective-permute-start(bf16[2,256,384]{2,1,0:T(8,128)(2,1)} %get-tuple-element.13), channel_id=1, source_target_pairs={{0,4},{2,6},{4,0},{6,2},{8,12},{10,14},{12,8},{14,10},{16,20},{18,... | collective-permute-start | bytes 1179656 | tf_op jit(solution)/shard_map/ppermute | solution.py:22
  22.0 0.0 collective-permute-start.5
  22.0 0.0 collective-permute-done.16
  22.0 0.0 copy-start
  22.0 0.0 copy-start.1
  22.1 0.0 copy-start.2
  22.1 0.0 copy-start.3
  22.1 0.0 copy-start.4
  22.1 0.3 collective-permute-start.1
  22.4 1.9 %collective-permute-done.17 = bf16[320,384]{1,0:T(8,128)(2,1)S(1)} collective-permute-done((bf16[320,384]{1,0:T(8,128)(2,1)S(1)}, bf16[320,384]{1,0:T(8,128)(2,1)S(1)}, u32[]{:S(2)}, u32[]{:S(2)}) %collective-permute-start.17) | collective-permute-done | bytes 245792 | tf_op jit(solution)/shard_map/ppermute | solution.py:22
  24.3 2.8 %collective-permute-done.14 = bf16[320,384]{1,0:T(8,128)(2,1)S(1)} collective-permute-done((bf16[320,384]{1,0:T(8,128)(2,1)}, bf16[320,384]{1,0:T(8,128)(2,1)S(1)}, u32[]{:S(2)}, u32[]{:S(2)}) %collective-permute-start.14) | collective-permute-done | bytes 245792 | tf_op jit(solution)/shard_map/ppermute | solution.py:22
  27.1 0.0 copy-done.5
  27.1 0.1 broadcast_select_fusion
  27.2 1.3 %collective-permute-start.21 = (bf16[2,320,384]{2,1,0:T(8,128)(2,1)S(1)}, bf16[2,320,384]{2,1,0:T(8,128)(2,1)S(1)}, u32[]{:S(2)}, u32[]{:S(2)}) collective-permute-start(bf16[2,320,384]{2,1,0:T(8,128)(2,1)S(1)} %get-tuple-element.19), channel_id=1, source_target_pairs={{0,1},{1,0},{2,3},{3,2},{4,5},{5,4},{6,7},{7,6},{8,9},{9,8},{10,11... | collective-permute-start | bytes 1474568 | tf_op jit(solution)/shard_map/ppermute | solution.py:26
  28.6 0.0 copy-done.6
  28.6 0.0 collective-permute-start
  28.6 3.8 %collective-permute-done.6.b2 = bf16[2,256,384]{2,1,0:T(8,128)(2,1)S(1)} collective-permute-done((bf16[2,256,384]{2,1,0:T(8,128)(2,1)}, bf16[2,256,384]{2,1,0:T(8,128)(2,1)S(1)}, u32[]{:S(2)}, u32[]{:S(2)}) %collective-permute-start.6) | collective-permute-done | bytes 393248 | tf_op jit(solution)/shard_map/ppermute | solution.py:22
  32.4 3.8 %collective-permute-start.8 = (bf16[2,256,384]{2,1,0:T(8,128)(2,1)S(1)}, bf16[2,256,384]{2,1,0:T(8,128)(2,1)S(1)}, u32[]{:S(2)}, u32[]{:S(2)}) collective-permute-start(bf16[2,256,384]{2,1,0:T(8,128)(2,1)S(1)} %collective-permute-done.6.b2), channel_id=1, source_target_pairs={{0,8},{2,10},{8,16},{10,18},{12,4},{14,6},{16,24},{18,26},{20,12},... | collective-permute-start | bytes 1179656 | tf_op jit(solution)/shard_map/ppermute | solution.py:22
  36.2 0.0 collective-permute-done.5.b1
  36.2 0.1 collective-permute-start.7
  36.3 1.7 %collective-permute-done.1.refs_7_ = bf16[2,256,384]{2,1,0:T(8,128)(2,1)S(1)} collective-permute-done((bf16[2,256,384]{2,1,0:T(8,128)(2,1)}, bf16[2,256,384]{2,1,0:T(8,128)(2,1)S(1)}, u32[]{:S(2)}, u32[]{:S(2)}) %collective-permute-start.1) | collective-permute-done | bytes 393248 | tf_op jit(solution)/shard_map/ppermute | solution.py:22
  38.0 5.3 %collective-permute-start.3 = (bf16[2,256,384]{2,1,0:T(8,128)(2,1)S(1)}, bf16[2,256,384]{2,1,0:T(8,128)(2,1)S(1)}, u32[]{:S(2)}, u32[]{:S(2)}) collective-permute-start(bf16[2,256,384]{2,1,0:T(8,128)(2,1)S(1)} %collective-permute-done.1.refs_7_), channel_id=1, source_target_pairs={{0,8},{2,10},{8,16},{10,18},{12,4},{14,6},{16,24},{18,26},{20,12},... | collective-permute-start | bytes 1179656 | tf_op jit(solution)/shard_map/ppermute | solution.py:22
  43.3 0.0 collective-permute-done.refs_6_
  43.3 0.1 collective-permute-start.19
  43.4 0.0 collective-permute-done.21.refs_21_
  43.4 2.0 %collective-permute-start.23 = (bf16[2,320,384]{2,1,0:T(8,128)(2,1)S(1)}, bf16[2,320,384]{2,1,0:T(8,128)(2,1)S(1)}, u32[]{:S(2)}, u32[]{:S(2)}) collective-permute-start(bf16[2,320,384]{2,1,0:T(8,128)(2,1)S(1)} %collective-permute-done.21.refs_21_), channel_id=1, source_target_pairs={{0,4},{2,6},{4,0},{6,2},{8,12},{10,14},{12,8},{14,10},{16,20},{18,... | collective-permute-start | bytes 1474568 | tf_op jit(solution)/shard_map/ppermute | solution.py:22
  45.4 0.0 collective-permute-done.8.b4
  45.4 0.0 collective-permute-start.2
  45.4 0.0 collective-permute-done.7.b3
  45.4 0.5 collective-permute-start.9
  45.9 5.6 %collective-permute-done.3.refs_9_ = bf16[2,256,384]{2,1,0:T(8,128)(2,1)S(1)} collective-permute-done((bf16[2,256,384]{2,1,0:T(8,128)(2,1)S(1)}, bf16[2,256,384]{2,1,0:T(8,128)(2,1)S(1)}, u32[]{:S(2)}, u32[]{:S(2)}) %collective-permute-start.3) | collective-permute-done | bytes 393248 | tf_op jit(solution)/shard_map/ppermute | solution.py:22
  51.5 0.0 collective-permute-start.18
  51.5 0.0 collective-permute-done.2.refs_8_
  51.5 0.5 collective-permute-start.22
  52.0 5.4 %collective-permute-done.19.refs_19_ = bf16[2,320,384]{2,1,0:T(8,128)(2,1)S(1)} collective-permute-done((bf16[2,320,384]{2,1,0:T(8,128)(2,1)S(1)}, bf16[2,320,384]{2,1,0:T(8,128)(2,1)S(1)}, u32[]{:S(2)}, u32[]{:S(2)}) %collective-permute-start.19) | collective-permute-done | bytes 491552 | tf_op jit(solution)/shard_map/ppermute | solution.py:22
  57.4 0.0 collective-permute-start.20
  57.4 8.1 %collective-permute-done.23.refs_23_ = bf16[2,320,384]{2,1,0:T(8,128)(2,1)S(1)} collective-permute-done((bf16[2,320,384]{2,1,0:T(8,128)(2,1)S(1)}, bf16[2,320,384]{2,1,0:T(8,128)(2,1)S(1)}, u32[]{:S(2)}, u32[]{:S(2)}) %collective-permute-start.23) | collective-permute-done | bytes 491552 | tf_op jit(solution)/shard_map/ppermute | solution.py:22
  65.5 0.0 collective-permute-start.24
  65.5 0.0 collective-permute-done.9.b5
  65.5 0.5 collective-permute-start.4
  66.0 0.0 copy-done
  66.0 0.0 copy-done.1
  66.1 3.4 %query_pass.1 = (bf16[256,384]{1,0:T(8,128)(2,1)S(1)}, f32[8,256]{1,0:T(8,128)S(1)}) custom-call(s32[1]{0:T(128)} %bitcast.at_ref.refs_0_, s32[32,128]{1,0:T(8,128)S(1)} %copy-done.4, bf16[256,384]{1,0:T(8,128)(2,1)S(1)} %copy-done.2, bf16[256,384]{1,0:T(8,128)(2,1)S(1)} %copy-done.3, bf16[256,384]{1,0:T(8,128)(2,1)S(1)} %copy-done, ...), custom_call_target="tpu_custom_call" | custom-call | tf_op jit(solution)/shard_map/query_pass/pallas_call | solution.py:226
  69.5 0.0 collective-permute-done.18.refs_18_
  69.5 0.1 collective-permute-start.10
  69.6 1.1 %collective-permute-done.10.refs_12_ = f32[8,256]{1,0:T(8,128)S(1)} collective-permute-done((f32[8,256]{1,0:T(8,128)S(1)}, f32[8,256]{1,0:T(8,128)S(1)}, u32[]{:S(2)}, u32[]{:S(2)}) %collective-permute-start.10) | collective-permute-done | bytes 8224 | tf_op jit(solution)/shard_map/ppermute | solution.py:22
  70.7 1.5 %collective-permute-start.13 = (bf16[256,384]{1,0:T(8,128)(2,1)S(1)}, bf16[256,384]{1,0:T(8,128)(2,1)S(1)}, u32[]{:S(2)}, u32[]{:S(2)}) collective-permute-start(bf16[256,384]{1,0:T(8,128)(2,1)S(1)} %get-tuple-element.15.refs_15_), channel_id=1, source_target_pairs={{0,1},{1,0},{2,3},{3,2},{4,5},{5,4},{6,7},{7,6},{8,9},{9,8},{10,11... | collective-permute-start | bytes 589832 | tf_op jit(solution)/shard_map/ppermute | solution.py:26
  72.2 0.0 collective-permute-done.4.refs_10_
  72.3 0.3 collective-permute-start.11
  72.5 3.5 %collective-permute-done.11.refs_13_ = f32[16,256]{1,0:T(8,128)S(1)} collective-permute-done((f32[16,256]{1,0:T(8,128)S(1)}, f32[16,256]{1,0:T(8,128)S(1)}, u32[]{:S(2)}, u32[]{:S(2)}) %collective-permute-start.11) | collective-permute-done | bytes 16416 | tf_op jit(solution)/shard_map/ppermute | solution.py:22
  76.0 1.9 %collective-permute-start.12 = (f32[16,256]{1,0:T(8,128)S(1)}, f32[16,256]{1,0:T(8,128)S(1)}, u32[]{:S(2)}, u32[]{:S(2)}) collective-permute-start(f32[16,256]{1,0:T(8,128)S(1)} %constant_dynamic-update-slice_fusion), channel_id=1, source_target_pairs={{4,8},{6,10},{8,4},{10,6},{12,16},{14,18},{16,12},{18,14},{20,24},... | collective-permute-start | bytes 49160 | tf_op jit(solution)/shard_map/ppermute | solution.py:22
  77.9 4.6 %collective-permute-done.12.refs_14_ = f32[16,256]{1,0:T(8,128)S(1)} collective-permute-done((f32[16,256]{1,0:T(8,128)S(1)}, f32[16,256]{1,0:T(8,128)S(1)}, u32[]{:S(2)}, u32[]{:S(2)}) %collective-permute-start.12) | collective-permute-done | bytes 16416 | tf_op jit(solution)/shard_map/ppermute | solution.py:22
  82.5 0.0 collective-permute-done.13.refs_16_
  82.5 0.0 collective-permute-done.20.refs_20_
  82.5 0.0 collective-permute-done.22.refs_22_
  82.5 0.0 collective-permute-done.24.refs_24_
  82.5 6.1 %final_pass.1 = (bf16[256,384]{1,0:T(8,128)(2,1)}, bf16[256,384]{1,0:T(8,128)(2,1)}, bf16[256,2560]{1,0:T(8,128)(2,1)}) custom-call(s32[1]{0:T(128)} %bitcast.at_ref.refs_0_, s32[32,128]{1,0:T(8,128)S(1)} %copy-done.4, bf16[256,384]{1,0:T(8,128)(2,1)S(1)} %copy-done, bf16[256,384]{1,0:T(8,128)(2,1)S(1)} %copy-done.1, bf16[256,384]{1,0:T(8,128)(2,1)S(1)} %copy-done.2, ...), custom_call_target="tpu_custom_call" | custom-call | tf_op jit(solution)/shard_map/final_pass/pallas_call | solution.py:321
  (7 shorter events, 0.0 us)
Async XLA Ops:
  0.6 26.4 %copy-start.5 = (bf16[320,384]{1,0:T(8,128)(2,1)S(1)}, bf16[320,384]{1,0:T(8,128)(2,1)}, u32[]{:S(2)}) copy-start(bf16[320,384]{1,0:T(8,128)(2,1)} %param.11) | copy-start | bytes 737284
  0.6 13.4 %collective-permute-start.15 = (bf16[320,384]{1,0:T(8,128)(2,1)}, bf16[320,384]{1,0:T(8,128)(2,1)S(1)}, u32[]{:S(2)}, u32[]{:S(2)}) collective-permute-start(bf16[320,384]{1,0:T(8,128)(2,1)} %param.11), channel_id=1, source_target_pairs={{0,16},{2,18},{4,20},{6,22},{8,24},{10,26},{12,28},{14,30},{16,0},... | collective-permute-start | bytes 737288 | tf_op jit(solution)/shard_map/ppermute | solution.py:22
  3.3 18.7 %collective-permute-start.16 = (bf16[320,384]{1,0:T(8,128)(2,1)}, bf16[320,384]{1,0:T(8,128)(2,1)S(1)}, u32[]{:S(2)}, u32[]{:S(2)}) collective-permute-start(bf16[320,384]{1,0:T(8,128)(2,1)} %param.11), channel_id=1, source_target_pairs={{8,16},{10,18},{12,20},{14,22},{16,8},{18,10},{20,12},{22,14},{9,1... | collective-permute-start | bytes 737288 | tf_op jit(solution)/shard_map/ppermute | solution.py:22
  14.1 10.2 %collective-permute-start.17 = (bf16[320,384]{1,0:T(8,128)(2,1)S(1)}, bf16[320,384]{1,0:T(8,128)(2,1)S(1)}, u32[]{:S(2)}, u32[]{:S(2)}) collective-permute-start(bf16[320,384]{1,0:T(8,128)(2,1)S(1)} %collective-permute-done.15), channel_id=1, source_target_pairs={{8,0},{10,2},{12,4},{14,6},{16,24},{18,26},{20,28},{22,30},{9,1},{... | collective-permute-start | bytes 737288 | tf_op jit(solution)/shard_map/ppermute | solution.py:22
  17.9 9.1 %collective-permute-start.14 = (bf16[320,384]{1,0:T(8,128)(2,1)}, bf16[320,384]{1,0:T(8,128)(2,1)S(1)}, u32[]{:S(2)}, u32[]{:S(2)}) collective-permute-start(bf16[320,384]{1,0:T(8,128)(2,1)} %param.11), channel_id=1, source_target_pairs={{0,8},{2,10},{4,12},{6,14},{8,0},{10,2},{12,4},{14,6},{16,24},{18,... | collective-permute-start | bytes 737288 | tf_op jit(solution)/shard_map/ppermute | solution.py:22
  20.2 12.2 %collective-permute-start.6 = (bf16[2,256,384]{2,1,0:T(8,128)(2,1)}, bf16[2,256,384]{2,1,0:T(8,128)(2,1)S(1)}, u32[]{:S(2)}, u32[]{:S(2)}) collective-permute-start(bf16[2,256,384]{2,1,0:T(8,128)(2,1)} %get-tuple-element.13), channel_id=1, source_target_pairs={{0,4},{2,6},{4,0},{6,2},{8,12},{10,14},{12,8},{14,10},{16,20},{18,... | collective-permute-start | bytes 1179656 | tf_op jit(solution)/shard_map/ppermute | solution.py:22
  22.0 14.2 %collective-permute-start.5 = (bf16[2,256,384]{2,1,0:T(8,128)(2,1)}, bf16[2,256,384]{2,1,0:T(8,128)(2,1)S(1)}, u32[]{:S(2)}, u32[]{:S(2)}) collective-permute-start(bf16[2,256,384]{2,1,0:T(8,128)(2,1)} %get-tuple-element.13), channel_id=1, source_target_pairs={{0,2},{2,0},{4,6},{6,4},{8,10},{10,8},{12,14},{14,12},{16,18},{18,... | collective-permute-start | bytes 1179656 | tf_op jit(solution)/shard_map/ppermute | solution.py:22
  22.0 6.5 %copy-start.6 = (bf16[2,256,384]{2,1,0:T(8,128)(2,1)S(1)}, bf16[2,256,384]{2,1,0:T(8,128)(2,1)}, u32[]{:S(2)}) copy-start(bf16[2,256,384]{2,1,0:T(8,128)(2,1)} %get-tuple-element.12) | copy-start | bytes 1179652
  22.0 44.0 %copy-start = (bf16[256,384]{1,0:T(8,128)(2,1)S(1)}, bf16[256,384]{1,0:T(8,128)(2,1)}, u32[]{:S(2)}) copy-start(bf16[256,384]{1,0:T(8,128)(2,1)} %refs_2_.1) | copy-start | bytes 589828
  22.0 44.0 %copy-start.1 = (bf16[256,384]{1,0:T(8,128)(2,1)S(1)}, bf16[256,384]{1,0:T(8,128)(2,1)}, u32[]{:S(2)}) copy-start(bf16[256,384]{1,0:T(8,128)(2,1)} %refs_3_.1) | copy-start | bytes 589828
  22.1 44.0 %copy-start.2 = (bf16[256,384]{1,0:T(8,128)(2,1)S(1)}, bf16[256,384]{1,0:T(8,128)(2,1)}, u32[]{:S(2)}) copy-start(bf16[256,384]{1,0:T(8,128)(2,1)} %refs_4_.1) | copy-start | bytes 589828
  22.1 44.0 %copy-start.3 = (bf16[256,384]{1,0:T(8,128)(2,1)S(1)}, bf16[256,384]{1,0:T(8,128)(2,1)}, u32[]{:S(2)}) copy-start(bf16[256,384]{1,0:T(8,128)(2,1)} %refs_5_.1) | copy-start | bytes 589828
  22.1 44.0 %copy-start.4 = (s32[32,128]{1,0:T(8,128)S(1)}, s32[32,128]{1,0:T(8,128)}, u32[]{:S(2)}) copy-start(s32[32,128]{1,0:T(8,128)} %get-tuple-element.11.lists_ref.refs_1_) | copy-start | bytes 49156
  22.1 15.9 %collective-permute-start.1 = (bf16[2,256,384]{2,1,0:T(8,128)(2,1)}, bf16[2,256,384]{2,1,0:T(8,128)(2,1)S(1)}, u32[]{:S(2)}, u32[]{:S(2)}) collective-permute-start(bf16[2,256,384]{2,1,0:T(8,128)(2,1)} %get-tuple-element.12), channel_id=1, source_target_pairs={{0,4},{2,6},{4,0},{6,2},{8,12},{10,14},{12,8},{14,10},{16,20},{18,... | collective-permute-start | bytes 1179656 | tf_op jit(solution)/shard_map/ppermute | solution.py:22
  27.2 16.2 %collective-permute-start.21 = (bf16[2,320,384]{2,1,0:T(8,128)(2,1)S(1)}, bf16[2,320,384]{2,1,0:T(8,128)(2,1)S(1)}, u32[]{:S(2)}, u32[]{:S(2)}) collective-permute-start(bf16[2,320,384]{2,1,0:T(8,128)(2,1)S(1)} %get-tuple-element.19), channel_id=1, source_target_pairs={{0,1},{1,0},{2,3},{3,2},{4,5},{5,4},{6,7},{7,6},{8,9},{9,8},{10,11... | collective-permute-start | bytes 1474568 | tf_op jit(solution)/shard_map/ppermute | solution.py:26
  28.6 14.7 %collective-permute-start = (bf16[2,256,384]{2,1,0:T(8,128)(2,1)S(1)}, bf16[2,256,384]{2,1,0:T(8,128)(2,1)S(1)}, u32[]{:S(2)}, u32[]{:S(2)}) collective-permute-start(bf16[2,256,384]{2,1,0:T(8,128)(2,1)S(1)} %copy-done.6), channel_id=1, source_target_pairs={{0,2},{2,0},{4,6},{6,4},{8,10},{10,8},{12,14},{14,12},{16,18},{18,... | collective-permute-start | bytes 1179656 | tf_op jit(solution)/shard_map/ppermute | solution.py:22
  32.4 13.0 %collective-permute-start.8 = (bf16[2,256,384]{2,1,0:T(8,128)(2,1)S(1)}, bf16[2,256,384]{2,1,0:T(8,128)(2,1)S(1)}, u32[]{:S(2)}, u32[]{:S(2)}) collective-permute-start(bf16[2,256,384]{2,1,0:T(8,128)(2,1)S(1)} %collective-permute-done.6.b2), channel_id=1, source_target_pairs={{0,8},{2,10},{8,16},{10,18},{12,4},{14,6},{16,24},{18,26},{20,12},... | collective-permute-start | bytes 1179656 | tf_op jit(solution)/shard_map/ppermute | solution.py:22
  36.2 9.2 %collective-permute-start.7 = (bf16[2,256,384]{2,1,0:T(8,128)(2,1)S(1)}, bf16[2,256,384]{2,1,0:T(8,128)(2,1)S(1)}, u32[]{:S(2)}, u32[]{:S(2)}) collective-permute-start(bf16[2,256,384]{2,1,0:T(8,128)(2,1)S(1)} %collective-permute-done.6.b2), channel_id=1, source_target_pairs={{0,2},{2,0},{4,6},{6,4},{8,10},{10,8},{12,14},{14,12},{16,18},{18,... | collective-permute-start | bytes 1179656 | tf_op jit(solution)/shard_map/ppermute | solution.py:22
  38.0 13.6 %collective-permute-start.3 = (bf16[2,256,384]{2,1,0:T(8,128)(2,1)S(1)}, bf16[2,256,384]{2,1,0:T(8,128)(2,1)S(1)}, u32[]{:S(2)}, u32[]{:S(2)}) collective-permute-start(bf16[2,256,384]{2,1,0:T(8,128)(2,1)S(1)} %collective-permute-done.1.refs_7_), channel_id=1, source_target_pairs={{0,8},{2,10},{8,16},{10,18},{12,4},{14,6},{16,24},{18,26},{20,12},... | collective-permute-start | bytes 1179656 | tf_op jit(solution)/shard_map/ppermute | solution.py:22
  43.3 14.2 %collective-permute-start.19 = (bf16[2,320,384]{2,1,0:T(8,128)(2,1)S(1)}, bf16[2,320,384]{2,1,0:T(8,128)(2,1)S(1)}, u32[]{:S(2)}, u32[]{:S(2)}) collective-permute-start(bf16[2,320,384]{2,1,0:T(8,128)(2,1)S(1)} %get-tuple-element.20.refs_17_), channel_id=1, source_target_pairs={{0,4},{2,6},{4,0},{6,2},{8,12},{10,14},{12,8},{14,10},{16,20},{18,... | collective-permute-start | bytes 1474568 | tf_op jit(solution)/shard_map/ppermute | solution.py:22
  43.4 22.1 %collective-permute-start.23 = (bf16[2,320,384]{2,1,0:T(8,128)(2,1)S(1)}, bf16[2,320,384]{2,1,0:T(8,128)(2,1)S(1)}, u32[]{:S(2)}, u32[]{:S(2)}) collective-permute-start(bf16[2,320,384]{2,1,0:T(8,128)(2,1)S(1)} %collective-permute-done.21.refs_21_), channel_id=1, source_target_pairs={{0,4},{2,6},{4,0},{6,2},{8,12},{10,14},{12,8},{14,10},{16,20},{18,... | collective-permute-start | bytes 1474568 | tf_op jit(solution)/shard_map/ppermute | solution.py:22
  45.4 6.2 %collective-permute-start.2 = (bf16[2,256,384]{2,1,0:T(8,128)(2,1)S(1)}, bf16[2,256,384]{2,1,0:T(8,128)(2,1)S(1)}, u32[]{:S(2)}, u32[]{:S(2)}) collective-permute-start(bf16[2,256,384]{2,1,0:T(8,128)(2,1)S(1)} %collective-permute-done.1.refs_7_), channel_id=1, source_target_pairs={{0,2},{2,0},{4,6},{6,4},{8,10},{10,8},{12,14},{14,12},{16,18},{18,... | collective-permute-start | bytes 1179656 | tf_op jit(solution)/shard_map/ppermute | solution.py:22
  45.4 20.1 %collective-permute-start.9 = (bf16[2,256,384]{2,1,0:T(8,128)(2,1)S(1)}, bf16[2,256,384]{2,1,0:T(8,128)(2,1)S(1)}, u32[]{:S(2)}, u32[]{:S(2)}) collective-permute-start(bf16[2,256,384]{2,1,0:T(8,128)(2,1)S(1)} %collective-permute-done.8.b4), channel_id=1, source_target_pairs={{0,2},{2,0},{4,6},{6,4},{8,10},{10,8},{12,14},{14,12},{16,18},{18,... | collective-permute-start | bytes 1179656 | tf_op jit(solution)/shard_map/ppermute | solution.py:22
  51.5 18.0 %collective-permute-start.18 = (bf16[2,320,384]{2,1,0:T(8,128)(2,1)S(1)}, bf16[2,320,384]{2,1,0:T(8,128)(2,1)S(1)}, u32[]{:S(2)}, u32[]{:S(2)}) collective-permute-start(bf16[2,320,384]{2,1,0:T(8,128)(2,1)S(1)} %get-tuple-element.20.refs_17_), channel_id=1, source_target_pairs={{0,2},{2,0},{4,6},{6,4},{8,10},{10,8},{12,14},{14,12},{16,18},{18,... | collective-permute-start | bytes 1474568 | tf_op jit(solution)/shard_map/ppermute | solution.py:22
  51.5 31.0 %collective-permute-start.22 = (bf16[2,320,384]{2,1,0:T(8,128)(2,1)S(1)}, bf16[2,320,384]{2,1,0:T(8,128)(2,1)S(1)}, u32[]{:S(2)}, u32[]{:S(2)}) collective-permute-start(bf16[2,320,384]{2,1,0:T(8,128)(2,1)S(1)} %collective-permute-done.21.refs_21_), channel_id=1, source_target_pairs={{0,2},{2,0},{4,6},{6,4},{8,10},{10,8},{12,14},{14,12},{16,18},{18,... | collective-permute-start | bytes 1474568 | tf_op jit(solution)/shard_map/ppermute | solution.py:22
  57.4 25.1 %collective-permute-start.20 = (bf16[2,320,384]{2,1,0:T(8,128)(2,1)S(1)}, bf16[2,320,384]{2,1,0:T(8,128)(2,1)S(1)}, u32[]{:S(2)}, u32[]{:S(2)}) collective-permute-start(bf16[2,320,384]{2,1,0:T(8,128)(2,1)S(1)} %collective-permute-done.19.refs_19_), channel_id=1, source_target_pairs={{0,2},{2,0},{4,6},{6,4},{8,10},{10,8},{12,14},{14,12},{16,18},{18,... | collective-permute-start | bytes 1474568 | tf_op jit(solution)/shard_map/ppermute | solution.py:22
  65.5 17.0 %collective-permute-start.24 = (bf16[2,320,384]{2,1,0:T(8,128)(2,1)S(1)}, bf16[2,320,384]{2,1,0:T(8,128)(2,1)S(1)}, u32[]{:S(2)}, u32[]{:S(2)}) collective-permute-start(bf16[2,320,384]{2,1,0:T(8,128)(2,1)S(1)} %collective-permute-done.23.refs_23_), channel_id=1, source_target_pairs={{0,2},{2,0},{4,6},{6,4},{8,10},{10,8},{12,14},{14,12},{16,18},{18,... | collective-permute-start | bytes 1474568 | tf_op jit(solution)/shard_map/ppermute | solution.py:22
  65.5 6.7 %collective-permute-start.4 = (bf16[2,256,384]{2,1,0:T(8,128)(2,1)S(1)}, bf16[2,256,384]{2,1,0:T(8,128)(2,1)S(1)}, u32[]{:S(2)}, u32[]{:S(2)}) collective-permute-start(bf16[2,256,384]{2,1,0:T(8,128)(2,1)S(1)} %collective-permute-done.3.refs_9_), channel_id=1, source_target_pairs={{0,2},{2,0},{4,6},{6,4},{8,10},{10,8},{12,14},{14,12},{16,18},{18,... | collective-permute-start | bytes 1179656 | tf_op jit(solution)/shard_map/ppermute | solution.py:22
  69.5 1.2 %collective-permute-start.10 = (f32[8,256]{1,0:T(8,128)S(1)}, f32[8,256]{1,0:T(8,128)S(1)}, u32[]{:S(2)}, u32[]{:S(2)}) collective-permute-start(f32[8,256]{1,0:T(8,128)S(1)} %get-tuple-element.14.refs_11_), channel_id=1, source_target_pairs={{0,2},{2,0},{4,6},{6,4},{8,10},{10,8},{12,14},{14,12},{16,18},{18,... | collective-permute-start | bytes 24584 | tf_op jit(solution)/shard_map/ppermute | solution.py:22
  70.7 11.8 %collective-permute-start.13 = (bf16[256,384]{1,0:T(8,128)(2,1)S(1)}, bf16[256,384]{1,0:T(8,128)(2,1)S(1)}, u32[]{:S(2)}, u32[]{:S(2)}) collective-permute-start(bf16[256,384]{1,0:T(8,128)(2,1)S(1)} %get-tuple-element.15.refs_15_), channel_id=1, source_target_pairs={{0,1},{1,0},{2,3},{3,2},{4,5},{5,4},{6,7},{7,6},{8,9},{9,8},{10,11... | collective-permute-start | bytes 589832 | tf_op jit(solution)/shard_map/ppermute | solution.py:26
  72.3 3.7 %collective-permute-start.11 = (f32[16,256]{1,0:T(8,128)S(1)}, f32[16,256]{1,0:T(8,128)S(1)}, u32[]{:S(2)}, u32[]{:S(2)}) collective-permute-start(f32[16,256]{1,0:T(8,128)S(1)} %constant_dynamic-update-slice_fusion), channel_id=1, source_target_pairs={{0,4},{2,6},{4,0},{6,2},{8,12},{10,14},{12,8},{14,10},{16,20},{18,... | collective-permute-start | bytes 49160 | tf_op jit(solution)/shard_map/ppermute | solution.py:22
  76.0 6.5 %collective-permute-start.12 = (f32[16,256]{1,0:T(8,128)S(1)}, f32[16,256]{1,0:T(8,128)S(1)}, u32[]{:S(2)}, u32[]{:S(2)}) collective-permute-start(f32[16,256]{1,0:T(8,128)S(1)} %constant_dynamic-update-slice_fusion), channel_id=1, source_target_pairs={{4,8},{6,10},{8,4},{10,6},{12,16},{14,18},{16,12},{18,14},{20,24},... | collective-permute-start | bytes 49160 | tf_op jit(solution)/shard_map/ppermute | solution.py:22

commit v3 on v2

--- a/solution.py
+++ b/solution.py
@@ -283,9 +283,10 @@
 def place_pieces(at_ref, pieces, w_ref):
     rows = pieces[0].shape[1]
     for j in range(2):
-        for i, piece in enumerate(pieces):
-            place = (at_ref[0] % 4) ^ (i % 4)
-            w_ref[j, i // 4, pl.ds(pl.multiple_of(place * rows, 64), rows)] = piece[j]
+        for i in range(4):
+            at = pl.ds(pl.multiple_of(((at_ref[0] % 4) ^ i) * rows, 64), rows)
+            w_ref[j, 0, at] = pieces[i][j]
+            w_ref[j, 1, at] = pieces[4 + 4 * j + i][...]
 
 
 def input_product(at_ref, q_ref, x_ref, w_ref, o_ref, out_ref, sems):
@@ -308,7 +309,7 @@
     at_ref = refs[0]
     key_args, refs = refs[:15], refs[15:]
     own_ref, other_ref = refs[:2]
-    pieces, refs = refs[2:10], refs[10:]
+    pieces, refs = refs[2:14], refs[14:]
     dk_ref, dv_ref, out_ref, mask_ref, w_ref, o_ref, sems = refs
     place_pieces(at_ref, pieces, w_ref)
     key_kernel(*key_args, dk_ref, dv_ref, mask_ref)
@@ -320,7 +321,7 @@
     span = pieces[0].shape[1] * 4
     return pl.pallas_call(
         final_kernel,
-        in_specs=[SMEM] + [VMEM] * 24,
+        in_specs=[SMEM] + [VMEM] * 28,
         out_specs=[VMEM, VMEM, ANYWHERE],
         out_shape=[jax.ShapeDtypeStruct((rows, width), jnp.bfloat16)] * 2
         + [jax.ShapeDtypeStruct((rows, 2 * span), jnp.bfloat16)],
@@ -345,13 +346,13 @@
     away = jnp.stack([by_two, by_three])
     same = position // 8 == group
     kept = jnp.where(same, near, away)
-    sent = jnp.where(same, away, near)
-    swapped = swap_groups(sent)
-    pieces = []
-    for held in (kept, swapped):
-        paired = move(held, to_frame_pair)
-        core = move(held, to_core)
-        pieces += [held, core, paired, move(paired, to_core)]
+    paired = move(kept, to_frame_pair)
+    pieces = [kept, move(kept, to_core), paired, move(paired, to_core)]
+    for j in range(2):
+        swapped = swap_groups(jnp.where(same, away[j], near[j]))
+        paired = move(swapped, to_frame_pair)
+        core = move(swapped, to_core)
+        pieces += [swapped, core, paired, move(paired, to_core)]
     return pieces
 
 

time: 88.9 us -> 75.1 us (0.84)
  waiting for transfers between devices: 47.4 us -> 28.9 us
  starting transfers between devices: 28.5 us -> 33.2 us
    ppermute x23 -> x26, waiting for transfers between devices: 47.4 us -> 24.3 us  [move(): lax.ppermute(block, 'seq', [(i, j) for i, j in pairs if 0 <= j < size])]
    ppermute x2 -> x3, waiting for transfers between devices: 0.01 us -> 4.59 us  [swap_groups(): return lax.ppermute(block, 'head', [(0, 1), (1, 0)])]
    ppermute x23 -> x26, starting transfers between devices: 25.6 us -> 28.2 us  [move(): lax.ppermute(block, 'seq', [(i, j) for i, j in pairs if 0 <= j < size])]
    ppermute x2 -> x3, starting transfers between devices: 2.85 us -> 4.99 us  [swap_groups(): return lax.ppermute(block, 'head', [(0, 1), (1, 0)])]
  transfers between devices with their start and end apart: 25 -> 29, of which waited for: 11 -> 9; matrix products, arithmetic and copies ran while one was open for 0% -> 0% of each run, Pallas kernels for 6% -> 8%
where the time goes in v3:
time: 75.1 us; the launch traced here: 74.8 us
  starting transfers between devices  33.2 us (44%)
  waiting for transfers between devices  28.9 us (38%)
  Pallas kernels  11.8 us (16%)
  between operations  0.85 us (1%)
    ppermute x26, starting transfers between devices, move(): lax.ppermute(block, 'seq', [(i, j) for i, j in pairs if 0 <= j < size])  28.2 us
    ppermute x26, waiting for transfers between devices, move(): lax.ppermute(block, 'seq', [(i, j) for i, j in pairs if 0 <= j < size])  24.3 us
    pallas_call x1, Pallas kernels, final_pass(): pl.pallas_call(final_kernel, in_specs=[SMEM] + [VMEM] * 28, out_specs=[VM...  6.11 us
    ppermute x3, starting transfers between devices, swap_groups(): return lax.ppermute(block, 'head', [(0, 1), (1, 0)])  4.99 us
    ppermute x3, waiting for transfers between devices, swap_groups(): return lax.ppermute(block, 'head', [(0, 1), (1, 0)])  4.59 us
    pallas_call x1, Pallas kernels, query_pass(): pl.pallas_call(query_kernel, in_specs=[SMEM] + [VMEM] * 10, out_specs=[VM...  3.44 us
    pallas_call x1, Pallas kernels, pack(): pl.pallas_call(pack_kernel, in_specs=[VMEM] * 6, out_specs=[VMEM] * 3, ou...  2.2 us
  transfers between devices with their start and end apart: 29, of which 9 were waited for; matrix products, arithmetic and copies ran while one was open for 0% of the time, Pallas kernels for 8%

profile of v3, /device:TPU:8, one launch (start us, length us, event | category | flops | bytes accessed | tf_op | source)
XLA Modules:
  0.0 74.8 jit_solution(2203553178617774147)
XLA Ops:
  0.6 2.7 %collective-permute-start.15 = (bf16[320,384]{1,0:T(8,128)(2,1)}, bf16[320,384]{1,0:T(8,128)(2,1)S(1)}, u32[]{:S(2)}, u32[]{:S(2)}) collective-permute-start(bf16[320,384]{1,0:T(8,128)(2,1)} %param.11), channel_id=1, source_target_pairs={{0,16},{2,18},{4,20},{6,22},{8,24},{10,26},{12,28},{14,30},{16,0},... | collective-permute-start | bytes 737288 | tf_op jit(solution)/shard_map/ppermute | solution.py:22
  3.3 0.4 collective-permute-start.14
  3.7 2.3 %collective-permute-start.16 = (bf16[320,384]{1,0:T(8,128)(2,1)}, bf16[320,384]{1,0:T(8,128)(2,1)S(1)}, u32[]{:S(2)}, u32[]{:S(2)}) collective-permute-start(bf16[320,384]{1,0:T(8,128)(2,1)} %param.11), channel_id=1, source_target_pairs={{8,16},{10,18},{12,20},{14,22},{16,8},{18,10},{20,12},{22,14},{9,1... | collective-permute-start | bytes 737288 | tf_op jit(solution)/shard_map/ppermute | solution.py:22
  6.1 0.0 copy-start.5
  6.1 2.2 %pack.1 = (bf16[2,256,384]{2,1,0:T(8,128)(2,1)}, bf16[2,256,384]{2,1,0:T(8,128)(2,1)}, s32[32,128]{1,0:T(8,128)}) custom-call(s32[12,32]{1,0:T(8,128)} %bitcast.11, s32[1,32]{1,0:T(1,128)} %bitcast.12, bf16[256,384]{1,0:T(8,128)(2,1)} %refs_2_.1, bf16[256,384]{1,0:T(8,128)(2,1)} %refs_3_.1, bf16[256,384]{1,0:T(8,128)(2,1)} %refs_4_.1, bf16[256,384]{1,0:T(8,128)(2,1)} %refs_5_.1), custom_call_target="tpu_custom_call" | custom-call | tf_op jit(solution)/shard_map/pack/pallas_call | solution.py:274
  8.3 1.5 %collective-permute-start.6 = (bf16[2,256,384]{2,1,0:T(8,128)(2,1)}, bf16[2,256,384]{2,1,0:T(8,128)(2,1)S(1)}, u32[]{:S(2)}, u32[]{:S(2)}) collective-permute-start(bf16[2,256,384]{2,1,0:T(8,128)(2,1)} %get-tuple-element.13), channel_id=1, source_target_pairs={{0,4},{2,6},{4,0},{6,2},{8,12},{10,14},{12,8},{14,10},{16,20},{18,... | collective-permute-start | bytes 1179656 | tf_op jit(solution)/shard_map/ppermute | solution.py:22
  9.8 4.2 %collective-permute-done.15 = bf16[320,384]{1,0:T(8,128)(2,1)S(1)} collective-permute-done((bf16[320,384]{1,0:T(8,128)(2,1)}, bf16[320,384]{1,0:T(8,128)(2,1)S(1)}, u32[]{:S(2)}, u32[]{:S(2)}) %collective-permute-start.15) | collective-permute-done | bytes 245792 | tf_op jit(solution)/shard_map/ppermute | solution.py:22
  14.1 3.9 %collective-permute-start.17 = (bf16[320,384]{1,0:T(8,128)(2,1)S(1)}, bf16[320,384]{1,0:T(8,128)(2,1)S(1)}, u32[]{:S(2)}, u32[]{:S(2)}) collective-permute-start(bf16[320,384]{1,0:T(8,128)(2,1)S(1)} %collective-permute-done.15), channel_id=1, source_target_pairs={{8,0},{10,2},{12,4},{14,6},{16,24},{18,26},{20,28},{22,30},{9,1},{... | collective-permute-start | bytes 737288 | tf_op jit(solution)/shard_map/ppermute | solution.py:22
  18.0 0.1 collective-permute-start.5
  18.1 0.0 collective-permute-done.14
  18.1 1.9 %collective-permute-start.1 = (bf16[2,256,384]{2,1,0:T(8,128)(2,1)}, bf16[2,256,384]{2,1,0:T(8,128)(2,1)S(1)}, u32[]{:S(2)}, u32[]{:S(2)}) collective-permute-start(bf16[2,256,384]{2,1,0:T(8,128)(2,1)} %get-tuple-element.12), channel_id=1, source_target_pairs={{0,4},{2,6},{4,0},{6,2},{8,12},{10,14},{12,8},{14,10},{16,20},{18,... | collective-permute-start | bytes 1179656 | tf_op jit(solution)/shard_map/ppermute | solution.py:22
  20.0 0.0 collective-permute-done.16
  20.0 0.1 collective-permute-start
  20.1 0.0 copy-start
  20.2 0.0 copy-start.1
  20.2 0.0 copy-start.2
  20.2 0.0 copy-start.3
  20.2 0.0 copy-start.4
  20.2 0.0 collective-permute-done.6.b2
  20.2 2.5 %collective-permute-start.21 = (bf16[320,384]{1,0:T(8,128)(2,1)S(1)}, bf16[320,384]{1,0:T(8,128)(2,1)S(1)}, u32[]{:S(2)}, u32[]{:S(2)}) collective-permute-start(bf16[320,384]{1,0:T(8,128)(2,1)S(1)} %broadcast_select_fusion.1), channel_id=1, source_target_pairs={{0,1},{1,0},{2,3},{3,2},{4,5},{5,4},{6,7},{7,6},{8,9},{9,8},{10,11... | collective-permute-start | bytes 737288 | tf_op jit(solution)/shard_map/ppermute | solution.py:26
  22.7 0.0 collective-permute-done.17
  22.7 4.3 %collective-permute-start.8 = (bf16[2,256,384]{2,1,0:T(8,128)(2,1)S(1)}, bf16[2,256,384]{2,1,0:T(8,128)(2,1)S(1)}, u32[]{:S(2)}, u32[]{:S(2)}) collective-permute-start(bf16[2,256,384]{2,1,0:T(8,128)(2,1)S(1)} %collective-permute-done.6.b2), channel_id=1, source_target_pairs={{0,8},{2,10},{8,16},{10,18},{12,4},{14,6},{16,24},{18,26},{20,12},... | collective-permute-start | bytes 1179656 | tf_op jit(solution)/shard_map/ppermute | solution.py:22
  27.0 0.1 broadcast_select_fusion
  27.1 0.0 collective-permute-done.5.b1
  27.1 1.6 %collective-permute-start.25 = (bf16[320,384]{1,0:T(8,128)(2,1)S(1)}, bf16[320,384]{1,0:T(8,128)(2,1)S(1)}, u32[]{:S(2)}, u32[]{:S(2)}) collective-permute-start(bf16[320,384]{1,0:T(8,128)(2,1)S(1)} %get-tuple-element.19), channel_id=1, source_target_pairs={{0,1},{1,0},{2,3},{3,2},{4,5},{5,4},{6,7},{7,6},{8,9},{9,8},{10,11... | collective-permute-start | bytes 737288 | tf_op jit(solution)/shard_map/ppermute | solution.py:26
  28.6 0.9 %collective-permute-done.21.refs_21_ = bf16[320,384]{1,0:T(8,128)(2,1)S(1)} collective-permute-done((bf16[320,384]{1,0:T(8,128)(2,1)S(1)}, bf16[320,384]{1,0:T(8,128)(2,1)S(1)}, u32[]{:S(2)}, u32[]{:S(2)}) %collective-permute-start.21) | collective-permute-done | bytes 245792 | tf_op jit(solution)/shard_map/ppermute | solution.py:26
  29.5 0.7 collective-permute-start.23
  30.2 0.0 collective-permute-done.1.refs_7_
  30.2 0.0 collective-permute-start.22
  30.2 0.0 collective-permute-done.refs_6_
  30.2 0.5 collective-permute-start.7
  30.7 0.1 maximum_select_fusion.refs_17_
  30.8 3.7 %collective-permute-done.25.refs_25_ = bf16[320,384]{1,0:T(8,128)(2,1)S(1)} collective-permute-done((bf16[320,384]{1,0:T(8,128)(2,1)S(1)}, bf16[320,384]{1,0:T(8,128)(2,1)S(1)}, u32[]{:S(2)}, u32[]{:S(2)}) %collective-permute-start.25) | collective-permute-done | bytes 245792 | tf_op jit(solution)/shard_map/ppermute | solution.py:26
  34.5 0.8 %collective-permute-start.19 = (bf16[2,320,384]{2,1,0:T(8,128)(2,1)S(1)}, bf16[2,320,384]{2,1,0:T(8,128)(2,1)S(1)}, u32[]{:S(2)}, u32[]{:S(2)}) collective-permute-start(bf16[2,320,384]{2,1,0:T(8,128)(2,1)S(1)} %maximum_select_fusion.refs_17_), channel_id=1, source_target_pairs={{0,4},{2,6},{4,0},{6,2},{8,12},{10,14},{12,8},{14,10},{16,20},{18,... | collective-permute-start | bytes 1474568 | tf_op jit(solution)/shard_map/ppermute | solution.py:22
  35.3 2.8 %collective-permute-done.23.refs_23_ = bf16[320,384]{1,0:T(8,128)(2,1)S(1)} collective-permute-done((bf16[320,384]{1,0:T(8,128)(2,1)S(1)}, bf16[320,384]{1,0:T(8,128)(2,1)S(1)}, u32[]{:S(2)}, u32[]{:S(2)}) %collective-permute-start.23) | collective-permute-done | bytes 245792 | tf_op jit(solution)/shard_map/ppermute | solution.py:22
  38.0 0.0 collective-permute-start.18
  38.1 0.0 collective-permute-done.22.refs_22_
  38.1 2.6 %collective-permute-start.3 = (bf16[2,256,384]{2,1,0:T(8,128)(2,1)S(1)}, bf16[2,256,384]{2,1,0:T(8,128)(2,1)S(1)}, u32[]{:S(2)}, u32[]{:S(2)}) collective-permute-start(bf16[2,256,384]{2,1,0:T(8,128)(2,1)S(1)} %collective-permute-done.1.refs_7_), channel_id=1, source_target_pairs={{0,8},{2,10},{8,16},{10,18},{12,4},{14,6},{16,24},{18,26},{20,12},... | collective-permute-start | bytes 1179656 | tf_op jit(solution)/shard_map/ppermute | solution.py:22
  40.7 0.0 collective-permute-done.8.b4
  40.7 0.3 collective-permute-start.2
  41.0 0.0 collective-permute-done.7.b3
  41.0 0.3 collective-permute-start.9
  41.3 10.2 %collective-permute-done.3.refs_9_ = bf16[2,256,384]{2,1,0:T(8,128)(2,1)S(1)} collective-permute-done((bf16[2,256,384]{2,1,0:T(8,128)(2,1)S(1)}, bf16[2,256,384]{2,1,0:T(8,128)(2,1)S(1)}, u32[]{:S(2)}, u32[]{:S(2)}) %collective-permute-start.3) | collective-permute-done | bytes 393248 | tf_op jit(solution)/shard_map/ppermute | solution.py:22
  51.5 1.0 %collective-permute-start.27 = (bf16[320,384]{1,0:T(8,128)(2,1)S(1)}, bf16[320,384]{1,0:T(8,128)(2,1)S(1)}, u32[]{:S(2)}, u32[]{:S(2)}) collective-permute-start(bf16[320,384]{1,0:T(8,128)(2,1)S(1)} %collective-permute-done.25.refs_25_), channel_id=1, source_target_pairs={{0,4},{2,6},{4,0},{6,2},{8,12},{10,14},{12,8},{14,10},{16,20},{18,... | collective-permute-start | bytes 737288 | tf_op jit(solution)/shard_map/ppermute | solution.py:22
  52.4 0.0 collective-permute-done.2.refs_8_
  52.4 0.0 collective-permute-start.26
  52.4 0.0 collective-permute-done.19.refs_19_
  52.4 0.5 collective-permute-start.20
  52.9 0.0 collective-permute-done.18.refs_18_
  52.9 0.1 collective-permute-start.4
  53.0 0.0 collective-permute-done.9.b5
  53.0 0.4 collective-permute-start.24
  53.5 3.4 %query_pass.1 = (bf16[256,384]{1,0:T(8,128)(2,1)S(1)}, f32[8,256]{1,0:T(8,128)S(1)}) custom-call(s32[1]{0:T(128)} %bitcast.at_ref.refs_0_, s32[32,128]{1,0:T(8,128)S(1)} %copy-done.4, bf16[256,384]{1,0:T(8,128)(2,1)S(1)} %copy-done.2, bf16[256,384]{1,0:T(8,128)(2,1)S(1)} %copy-done.3, bf16[256,384]{1,0:T(8,128)(2,1)S(1)} %copy-done, ...), custom_call_target="tpu_custom_call" | custom-call | tf_op jit(solution)/shard_map/query_pass/pallas_call | solution.py:226
  56.9 2.0 %collective-permute-done.27.refs_27_ = bf16[320,384]{1,0:T(8,128)(2,1)S(1)} collective-permute-done((bf16[320,384]{1,0:T(8,128)(2,1)S(1)}, bf16[320,384]{1,0:T(8,128)(2,1)S(1)}, u32[]{:S(2)}, u32[]{:S(2)}) %collective-permute-start.27) | collective-permute-done | bytes 245792 | tf_op jit(solution)/shard_map/ppermute | solution.py:22
  59.0 0.5 collective-permute-start.28
  59.5 0.7 collective-permute-done.10.refs_12_
  60.1 0.9 %collective-permute-start.13 = (bf16[256,384]{1,0:T(8,128)(2,1)S(1)}, bf16[256,384]{1,0:T(8,128)(2,1)S(1)}, u32[]{:S(2)}, u32[]{:S(2)}) collective-permute-start(bf16[256,384]{1,0:T(8,128)(2,1)S(1)} %get-tuple-element.15.refs_15_), channel_id=1, source_target_pairs={{0,1},{1,0},{2,3},{3,2},{4,5},{5,4},{6,7},{7,6},{8,9},{9,8},{10,11... | collective-permute-start | bytes 589832 | tf_op jit(solution)/shard_map/ppermute | solution.py:26
  61.1 0.0 collective-permute-done.24.refs_24_
  61.1 1.1 %collective-permute-start.11 = (f32[16,256]{1,0:T(8,128)S(1)}, f32[16,256]{1,0:T(8,128)S(1)}, u32[]{:S(2)}, u32[]{:S(2)}) collective-permute-start(f32[16,256]{1,0:T(8,128)S(1)} %constant_dynamic-update-slice_fusion), channel_id=1, source_target_pairs={{0,4},{2,6},{4,0},{6,2},{8,12},{10,14},{12,8},{14,10},{16,20},{18,... | collective-permute-start | bytes 49160 | tf_op jit(solution)/shard_map/ppermute | solution.py:22
  62.2 0.0 collective-permute-done.4.refs_10_
  62.2 2.2 %collective-permute-start.12 = (f32[16,256]{1,0:T(8,128)S(1)}, f32[16,256]{1,0:T(8,128)S(1)}, u32[]{:S(2)}, u32[]{:S(2)}) collective-permute-start(f32[16,256]{1,0:T(8,128)S(1)} %constant_dynamic-update-slice_fusion), channel_id=1, source_target_pairs={{4,8},{6,10},{8,4},{10,6},{12,16},{14,18},{16,12},{18,14},{20,24},... | collective-permute-start | bytes 49160 | tf_op jit(solution)/shard_map/ppermute | solution.py:22
  64.4 0.4 collective-permute-done.11.refs_13_
  64.8 3.9 %collective-permute-done.12.refs_14_ = f32[16,256]{1,0:T(8,128)S(1)} collective-permute-done((f32[16,256]{1,0:T(8,128)S(1)}, f32[16,256]{1,0:T(8,128)S(1)}, u32[]{:S(2)}, u32[]{:S(2)}) %collective-permute-start.12) | collective-permute-done | bytes 16416 | tf_op jit(solution)/shard_map/ppermute | solution.py:22
  68.7 6.1 %final_pass.1 = (bf16[256,384]{1,0:T(8,128)(2,1)}, bf16[256,384]{1,0:T(8,128)(2,1)}, bf16[256,2560]{1,0:T(8,128)(2,1)}) custom-call(s32[1]{0:T(128)} %bitcast.at_ref.refs_0_, s32[32,128]{1,0:T(8,128)S(1)} %copy-done.4, bf16[256,384]{1,0:T(8,128)(2,1)S(1)} %copy-done, bf16[256,384]{1,0:T(8,128)(2,1)S(1)} %copy-done.1, bf16[256,384]{1,0:T(8,128)(2,1)S(1)} %copy-done.2, ...), custom_call_target="tpu_custom_call" | custom-call | tf_op jit(solution)/shard_map/final_pass/pallas_call | solution.py:322
  (14 shorter events, 0.1 us)
Async XLA Ops:
  0.6 13.4 %collective-permute-start.15 = (bf16[320,384]{1,0:T(8,128)(2,1)}, bf16[320,384]{1,0:T(8,128)(2,1)S(1)}, u32[]{:S(2)}, u32[]{:S(2)}) collective-permute-start(bf16[320,384]{1,0:T(8,128)(2,1)} %param.11), channel_id=1, source_target_pairs={{0,16},{2,18},{4,20},{6,22},{8,24},{10,26},{12,28},{14,30},{16,0},... | collective-permute-start | bytes 737288 | tf_op jit(solution)/shard_map/ppermute | solution.py:22
  3.3 14.8 %collective-permute-start.14 = (bf16[320,384]{1,0:T(8,128)(2,1)}, bf16[320,384]{1,0:T(8,128)(2,1)S(1)}, u32[]{:S(2)}, u32[]{:S(2)}) collective-permute-start(bf16[320,384]{1,0:T(8,128)(2,1)} %param.11), channel_id=1, source_target_pairs={{0,8},{2,10},{4,12},{6,14},{8,0},{10,2},{12,4},{14,6},{16,24},{18,... | collective-permute-start | bytes 737288 | tf_op jit(solution)/shard_map/ppermute | solution.py:22
  3.7 16.2 %collective-permute-start.16 = (bf16[320,384]{1,0:T(8,128)(2,1)}, bf16[320,384]{1,0:T(8,128)(2,1)S(1)}, u32[]{:S(2)}, u32[]{:S(2)}) collective-permute-start(bf16[320,384]{1,0:T(8,128)(2,1)} %param.11), channel_id=1, source_target_pairs={{8,16},{10,18},{12,20},{14,22},{16,8},{18,10},{20,12},{22,14},{9,1... | collective-permute-start | bytes 737288 | tf_op jit(solution)/shard_map/ppermute | solution.py:22
  6.1 24.6 %copy-start.5 = (bf16[320,384]{1,0:T(8,128)(2,1)S(1)}, bf16[320,384]{1,0:T(8,128)(2,1)}, u32[]{:S(2)}) copy-start(bf16[320,384]{1,0:T(8,128)(2,1)} %param.11) | copy-start | bytes 737284
  8.3 11.9 %collective-permute-start.6 = (bf16[2,256,384]{2,1,0:T(8,128)(2,1)}, bf16[2,256,384]{2,1,0:T(8,128)(2,1)S(1)}, u32[]{:S(2)}, u32[]{:S(2)}) collective-permute-start(bf16[2,256,384]{2,1,0:T(8,128)(2,1)} %get-tuple-element.13), channel_id=1, source_target_pairs={{0,4},{2,6},{4,0},{6,2},{8,12},{10,14},{12,8},{14,10},{16,20},{18,... | collective-permute-start | bytes 1179656 | tf_op jit(solution)/shard_map/ppermute | solution.py:22
  14.1 8.7 %collective-permute-start.17 = (bf16[320,384]{1,0:T(8,128)(2,1)S(1)}, bf16[320,384]{1,0:T(8,128)(2,1)S(1)}, u32[]{:S(2)}, u32[]{:S(2)}) collective-permute-start(bf16[320,384]{1,0:T(8,128)(2,1)S(1)} %collective-permute-done.15), channel_id=1, source_target_pairs={{8,0},{10,2},{12,4},{14,6},{16,24},{18,26},{20,28},{22,30},{9,1},{... | collective-permute-start | bytes 737288 | tf_op jit(solution)/shard_map/ppermute | solution.py:22
  18.0 9.1 %collective-permute-start.5 = (bf16[2,256,384]{2,1,0:T(8,128)(2,1)}, bf16[2,256,384]{2,1,0:T(8,128)(2,1)S(1)}, u32[]{:S(2)}, u32[]{:S(2)}) collective-permute-start(bf16[2,256,384]{2,1,0:T(8,128)(2,1)} %get-tuple-element.13), channel_id=1, source_target_pairs={{0,2},{2,0},{4,6},{6,4},{8,10},{10,8},{12,14},{14,12},{16,18},{18,... | collective-permute-start | bytes 1179656 | tf_op jit(solution)/shard_map/ppermute | solution.py:22
  18.1 12.1 %collective-permute-start.1 = (bf16[2,256,384]{2,1,0:T(8,128)(2,1)}, bf16[2,256,384]{2,1,0:T(8,128)(2,1)S(1)}, u32[]{:S(2)}, u32[]{:S(2)}) collective-permute-start(bf16[2,256,384]{2,1,0:T(8,128)(2,1)} %get-tuple-element.12), channel_id=1, source_target_pairs={{0,4},{2,6},{4,0},{6,2},{8,12},{10,14},{12,8},{14,10},{16,20},{18,... | collective-permute-start | bytes 1179656 | tf_op jit(solution)/shard_map/ppermute | solution.py:22
  20.0 10.2 %collective-permute-start = (bf16[2,256,384]{2,1,0:T(8,128)(2,1)}, bf16[2,256,384]{2,1,0:T(8,128)(2,1)S(1)}, u32[]{:S(2)}, u32[]{:S(2)}) collective-permute-start(bf16[2,256,384]{2,1,0:T(8,128)(2,1)} %get-tuple-element.12), channel_id=1, source_target_pairs={{0,2},{2,0},{4,6},{6,4},{8,10},{10,8},{12,14},{14,12},{16,18},{18,... | collective-permute-start | bytes 1179656 | tf_op jit(solution)/shard_map/ppermute | solution.py:22
  20.1 33.3 %copy-start = (bf16[256,384]{1,0:T(8,128)(2,1)S(1)}, bf16[256,384]{1,0:T(8,128)(2,1)}, u32[]{:S(2)}) copy-start(bf16[256,384]{1,0:T(8,128)(2,1)} %refs_2_.1) | copy-start | bytes 589828
  20.2 33.3 %copy-start.1 = (bf16[256,384]{1,0:T(8,128)(2,1)S(1)}, bf16[256,384]{1,0:T(8,128)(2,1)}, u32[]{:S(2)}) copy-start(bf16[256,384]{1,0:T(8,128)(2,1)} %refs_3_.1) | copy-start | bytes 589828
  20.2 33.3 %copy-start.2 = (bf16[256,384]{1,0:T(8,128)(2,1)S(1)}, bf16[256,384]{1,0:T(8,128)(2,1)}, u32[]{:S(2)}) copy-start(bf16[256,384]{1,0:T(8,128)(2,1)} %refs_4_.1) | copy-start | bytes 589828
  20.2 33.3 %copy-start.3 = (bf16[256,384]{1,0:T(8,128)(2,1)S(1)}, bf16[256,384]{1,0:T(8,128)(2,1)}, u32[]{:S(2)}) copy-start(bf16[256,384]{1,0:T(8,128)(2,1)} %refs_5_.1) | copy-start | bytes 589828
  20.2 33.3 %copy-start.4 = (s32[32,128]{1,0:T(8,128)S(1)}, s32[32,128]{1,0:T(8,128)}, u32[]{:S(2)}) copy-start(s32[32,128]{1,0:T(8,128)} %get-tuple-element.11.lists_ref.refs_1_) | copy-start | bytes 49156
  20.2 9.3 %collective-permute-start.21 = (bf16[320,384]{1,0:T(8,128)(2,1)S(1)}, bf16[320,384]{1,0:T(8,128)(2,1)S(1)}, u32[]{:S(2)}, u32[]{:S(2)}) collective-permute-start(bf16[320,384]{1,0:T(8,128)(2,1)S(1)} %broadcast_select_fusion.1), channel_id=1, source_target_pairs={{0,1},{1,0},{2,3},{3,2},{4,5},{5,4},{6,7},{7,6},{8,9},{9,8},{10,11... | collective-permute-start | bytes 737288 | tf_op jit(solution)/shard_map/ppermute | solution.py:26
  22.7 18.0 %collective-permute-start.8 = (bf16[2,256,384]{2,1,0:T(8,128)(2,1)S(1)}, bf16[2,256,384]{2,1,0:T(8,128)(2,1)S(1)}, u32[]{:S(2)}, u32[]{:S(2)}) collective-permute-start(bf16[2,256,384]{2,1,0:T(8,128)(2,1)S(1)} %collective-permute-done.6.b2), channel_id=1, source_target_pairs={{0,8},{2,10},{8,16},{10,18},{12,4},{14,6},{16,24},{18,26},{20,12},... | collective-permute-start | bytes 1179656 | tf_op jit(solution)/shard_map/ppermute | solution.py:22
  27.1 7.4 %collective-permute-start.25 = (bf16[320,384]{1,0:T(8,128)(2,1)S(1)}, bf16[320,384]{1,0:T(8,128)(2,1)S(1)}, u32[]{:S(2)}, u32[]{:S(2)}) collective-permute-start(bf16[320,384]{1,0:T(8,128)(2,1)S(1)} %get-tuple-element.19), channel_id=1, source_target_pairs={{0,1},{1,0},{2,3},{3,2},{4,5},{5,4},{6,7},{7,6},{8,9},{9,8},{10,11... | collective-permute-start | bytes 737288 | tf_op jit(solution)/shard_map/ppermute | solution.py:26
  29.5 8.5 %collective-permute-start.23 = (bf16[320,384]{1,0:T(8,128)(2,1)S(1)}, bf16[320,384]{1,0:T(8,128)(2,1)S(1)}, u32[]{:S(2)}, u32[]{:S(2)}) collective-permute-start(bf16[320,384]{1,0:T(8,128)(2,1)S(1)} %collective-permute-done.21.refs_21_), channel_id=1, source_target_pairs={{0,4},{2,6},{4,0},{6,2},{8,12},{10,14},{12,8},{14,10},{16,20},{18,... | collective-permute-start | bytes 737288 | tf_op jit(solution)/shard_map/ppermute | solution.py:22
  30.2 7.9 %collective-permute-start.22 = (bf16[320,384]{1,0:T(8,128)(2,1)S(1)}, bf16[320,384]{1,0:T(8,128)(2,1)S(1)}, u32[]{:S(2)}, u32[]{:S(2)}) collective-permute-start(bf16[320,384]{1,0:T(8,128)(2,1)S(1)} %collective-permute-done.21.refs_21_), channel_id=1, source_target_pairs={{0,2},{2,0},{4,6},{6,4},{8,10},{10,8},{12,14},{14,12},{16,18},{18,... | collective-permute-start | bytes 737288 | tf_op jit(solution)/shard_map/ppermute | solution.py:22
  30.2 10.8 %collective-permute-start.7 = (bf16[2,256,384]{2,1,0:T(8,128)(2,1)S(1)}, bf16[2,256,384]{2,1,0:T(8,128)(2,1)S(1)}, u32[]{:S(2)}, u32[]{:S(2)}) collective-permute-start(bf16[2,256,384]{2,1,0:T(8,128)(2,1)S(1)} %collective-permute-done.6.b2), channel_id=1, source_target_pairs={{0,2},{2,0},{4,6},{6,4},{8,10},{10,8},{12,14},{14,12},{16,18},{18,... | collective-permute-start | bytes 1179656 | tf_op jit(solution)/shard_map/ppermute | solution.py:22
  34.5 17.9 %collective-permute-start.19 = (bf16[2,320,384]{2,1,0:T(8,128)(2,1)S(1)}, bf16[2,320,384]{2,1,0:T(8,128)(2,1)S(1)}, u32[]{:S(2)}, u32[]{:S(2)}) collective-permute-start(bf16[2,320,384]{2,1,0:T(8,128)(2,1)S(1)} %maximum_select_fusion.refs_17_), channel_id=1, source_target_pairs={{0,4},{2,6},{4,0},{6,2},{8,12},{10,14},{12,8},{14,10},{16,20},{18,... | collective-permute-start | bytes 1474568 | tf_op jit(solution)/shard_map/ppermute | solution.py:22
  38.0 14.9 %collective-permute-start.18 = (bf16[2,320,384]{2,1,0:T(8,128)(2,1)S(1)}, bf16[2,320,384]{2,1,0:T(8,128)(2,1)S(1)}, u32[]{:S(2)}, u32[]{:S(2)}) collective-permute-start(bf16[2,320,384]{2,1,0:T(8,128)(2,1)S(1)} %maximum_select_fusion.refs_17_), channel_id=1, source_target_pairs={{0,2},{2,0},{4,6},{6,4},{8,10},{10,8},{12,14},{14,12},{16,18},{18,... | collective-permute-start | bytes 1474568 | tf_op jit(solution)/shard_map/ppermute | solution.py:22
  38.1 13.4 %collective-permute-start.3 = (bf16[2,256,384]{2,1,0:T(8,128)(2,1)S(1)}, bf16[2,256,384]{2,1,0:T(8,128)(2,1)S(1)}, u32[]{:S(2)}, u32[]{:S(2)}) collective-permute-start(bf16[2,256,384]{2,1,0:T(8,128)(2,1)S(1)} %collective-permute-done.1.refs_7_), channel_id=1, source_target_pairs={{0,8},{2,10},{8,16},{10,18},{12,4},{14,6},{16,24},{18,26},{20,12},... | collective-permute-start | bytes 1179656 | tf_op jit(solution)/shard_map/ppermute | solution.py:22
  40.7 11.7 %collective-permute-start.2 = (bf16[2,256,384]{2,1,0:T(8,128)(2,1)S(1)}, bf16[2,256,384]{2,1,0:T(8,128)(2,1)S(1)}, u32[]{:S(2)}, u32[]{:S(2)}) collective-permute-start(bf16[2,256,384]{2,1,0:T(8,128)(2,1)S(1)} %collective-permute-done.1.refs_7_), channel_id=1, source_target_pairs={{0,2},{2,0},{4,6},{6,4},{8,10},{10,8},{12,14},{14,12},{16,18},{18,... | collective-permute-start | bytes 1179656 | tf_op jit(solution)/shard_map/ppermute | solution.py:22
  41.0 12.0 %collective-permute-start.9 = (bf16[2,256,384]{2,1,0:T(8,128)(2,1)S(1)}, bf16[2,256,384]{2,1,0:T(8,128)(2,1)S(1)}, u32[]{:S(2)}, u32[]{:S(2)}) collective-permute-start(bf16[2,256,384]{2,1,0:T(8,128)(2,1)S(1)} %collective-permute-done.8.b4), channel_id=1, source_target_pairs={{0,2},{2,0},{4,6},{6,4},{8,10},{10,8},{12,14},{14,12},{16,18},{18,... | collective-permute-start | bytes 1179656 | tf_op jit(solution)/shard_map/ppermute | solution.py:22
  51.5 7.5 %collective-permute-start.27 = (bf16[320,384]{1,0:T(8,128)(2,1)S(1)}, bf16[320,384]{1,0:T(8,128)(2,1)S(1)}, u32[]{:S(2)}, u32[]{:S(2)}) collective-permute-start(bf16[320,384]{1,0:T(8,128)(2,1)S(1)} %collective-permute-done.25.refs_25_), channel_id=1, source_target_pairs={{0,4},{2,6},{4,0},{6,2},{8,12},{10,14},{12,8},{14,10},{16,20},{18,... | collective-permute-start | bytes 737288 | tf_op jit(solution)/shard_map/ppermute | solution.py:22
  52.4 6.5 %collective-permute-start.26 = (bf16[320,384]{1,0:T(8,128)(2,1)S(1)}, bf16[320,384]{1,0:T(8,128)(2,1)S(1)}, u32[]{:S(2)}, u32[]{:S(2)}) collective-permute-start(bf16[320,384]{1,0:T(8,128)(2,1)S(1)} %collective-permute-done.25.refs_25_), channel_id=1, source_target_pairs={{0,2},{2,0},{4,6},{6,4},{8,10},{10,8},{12,14},{14,12},{16,18},{18,... | collective-permute-start | bytes 737288 | tf_op jit(solution)/shard_map/ppermute | solution.py:22
  52.4 16.3 %collective-permute-start.20 = (bf16[2,320,384]{2,1,0:T(8,128)(2,1)S(1)}, bf16[2,320,384]{2,1,0:T(8,128)(2,1)S(1)}, u32[]{:S(2)}, u32[]{:S(2)}) collective-permute-start(bf16[2,320,384]{2,1,0:T(8,128)(2,1)S(1)} %collective-permute-done.19.refs_19_), channel_id=1, source_target_pairs={{0,2},{2,0},{4,6},{6,4},{8,10},{10,8},{12,14},{14,12},{16,18},{18,... | collective-permute-start | bytes 1474568 | tf_op jit(solution)/shard_map/ppermute | solution.py:22
  52.9 9.2 %collective-permute-start.4 = (bf16[2,256,384]{2,1,0:T(8,128)(2,1)S(1)}, bf16[2,256,384]{2,1,0:T(8,128)(2,1)S(1)}, u32[]{:S(2)}, u32[]{:S(2)}) collective-permute-start(bf16[2,256,384]{2,1,0:T(8,128)(2,1)S(1)} %collective-permute-done.3.refs_9_), channel_id=1, source_target_pairs={{0,2},{2,0},{4,6},{6,4},{8,10},{10,8},{12,14},{14,12},{16,18},{18,... | collective-permute-start | bytes 1179656 | tf_op jit(solution)/shard_map/ppermute | solution.py:22
  53.0 8.1 %collective-permute-start.24 = (bf16[320,384]{1,0:T(8,128)(2,1)S(1)}, bf16[320,384]{1,0:T(8,128)(2,1)S(1)}, u32[]{:S(2)}, u32[]{:S(2)}) collective-permute-start(bf16[320,384]{1,0:T(8,128)(2,1)S(1)} %collective-permute-done.23.refs_23_), channel_id=1, source_target_pairs={{0,2},{2,0},{4,6},{6,4},{8,10},{10,8},{12,14},{14,12},{16,18},{18,... | collective-permute-start | bytes 737288 | tf_op jit(solution)/shard_map/ppermute | solution.py:22
  59.0 1.2 %collective-permute-start.10 = (f32[8,256]{1,0:T(8,128)S(1)}, f32[8,256]{1,0:T(8,128)S(1)}, u32[]{:S(2)}, u32[]{:S(2)}) collective-permute-start(f32[8,256]{1,0:T(8,128)S(1)} %get-tuple-element.14.refs_11_), channel_id=1, source_target_pairs={{0,2},{2,0},{4,6},{6,4},{8,10},{10,8},{12,14},{14,12},{16,18},{18,... | collective-permute-start | bytes 24584 | tf_op jit(solution)/shard_map/ppermute | solution.py:22
  59.0 9.7 %collective-permute-start.28 = (bf16[320,384]{1,0:T(8,128)(2,1)S(1)}, bf16[320,384]{1,0:T(8,128)(2,1)S(1)}, u32[]{:S(2)}, u32[]{:S(2)}) collective-permute-start(bf16[320,384]{1,0:T(8,128)(2,1)S(1)} %collective-permute-done.27.refs_27_), channel_id=1, source_target_pairs={{0,2},{2,0},{4,6},{6,4},{8,10},{10,8},{12,14},{14,12},{16,18},{18,... | collective-permute-start | bytes 737288 | tf_op jit(solution)/shard_map/ppermute | solution.py:22
  60.1 8.6 %collective-permute-start.13 = (bf16[256,384]{1,0:T(8,128)(2,1)S(1)}, bf16[256,384]{1,0:T(8,128)(2,1)S(1)}, u32[]{:S(2)}, u32[]{:S(2)}) collective-permute-start(bf16[256,384]{1,0:T(8,128)(2,1)S(1)} %get-tuple-element.15.refs_15_), channel_id=1, source_target_pairs={{0,1},{1,0},{2,3},{3,2},{4,5},{5,4},{6,7},{7,6},{8,9},{9,8},{10,11... | collective-permute-start | bytes 589832 | tf_op jit(solution)/shard_map/ppermute | solution.py:26
  61.1 3.7 %collective-permute-start.11 = (f32[16,256]{1,0:T(8,128)S(1)}, f32[16,256]{1,0:T(8,128)S(1)}, u32[]{:S(2)}, u32[]{:S(2)}) collective-permute-start(f32[16,256]{1,0:T(8,128)S(1)} %constant_dynamic-update-slice_fusion), channel_id=1, source_target_pairs={{0,4},{2,6},{4,0},{6,2},{8,12},{10,14},{12,8},{14,10},{16,20},{18,... | collective-permute-start | bytes 49160 | tf_op jit(solution)/shard_map/ppermute | solution.py:22
  62.2 6.5 %collective-permute-start.12 = (f32[16,256]{1,0:T(8,128)S(1)}, f32[16,256]{1,0:T(8,128)S(1)}, u32[]{:S(2)}, u32[]{:S(2)}) collective-permute-start(f32[16,256]{1,0:T(8,128)S(1)} %constant_dynamic-update-slice_fusion), channel_id=1, source_target_pairs={{4,8},{6,10},{8,4},{10,6},{12,16},{14,18},{16,12},{18,14},{20,24},... | collective-permute-start | bytes 49160 | tf_op jit(solution)/shard_map/ppermute | solution.py:22
